TPU v7x, 128 devices: a whole 4x4x4 slice. The times are simulated.
128 devices in a mesh: index: 8 (over y, core), bulk: 16 (over z, x).
Axes of the slice: x: 4, y: 4, z: 4, core: 2. Of those that a mesh axis runs over, the one named last changes fastest.
Arguments:
- questions: bfloat16 [4096, 768], P(('index', 'bulk')), may hold values from -26 to 26
- passages: bfloat16 [262144, 768], P(('index', 'bulk')), may hold values from -6 to 6
- candidate_ids: int32 [4096, 32], P(('index', 'bulk')), may hold values from 0 to 262143, as said below
- reader_loglik: float32 [4096, 32], P(('index', 'bulk')), may hold values from -400 to 0
Outputs:
- mean_divergence: float32 [], replicated
- question_grads: float32 [4096, 768], P(('index', 'bulk'))
Inputs may be any that keep to these rules, and one draw needn't show every extreme that they name: `candidate_ids`: passage id p lies in the range of owner p // 2048. Among the 32 candidates of the 32 questions of one device, at most 16 lie in one owner's range; in every draw some owner has exactly 16 from every device, and every owner has at least one from every device.
All inputs are finite; a program needn't handle non-finite values.
Results may differ from a plain program's by a relative error of at most 0.0024.
Values may be sent and summed in bfloat16 or wider, within the bound.
No kernel may reach another device: no remote copies, remote signals or barrier semaphores. Data moves between devices by JAX's collectives and lax.ppermute only.
A program may use at most 64 MiB of HBM per device.

v0:
```python
import math

import jax
import jax.numpy as jnp
from jax import lax
from jax.sharding import PartitionSpec as P


def log_normalize(logits):
    highest = jnp.max(logits, axis=1, keepdims=True)
    shifted = logits - highest
    return shifted - jnp.log(jnp.sum(jnp.exp(shifted), axis=1, keepdims=True))


def send_requests(request):
    return lax.all_to_all(request, ("index", "bulk"), split_axis=0, concat_axis=0, tiled=True)


def return_rows(fetched):
    return lax.all_to_all(fetched, ("index", "bulk"), split_axis=0, concat_axis=0, tiled=True)


def body(questions, passages, candidate_ids, reader_loglik):
    owners = lax.axis_size(("index", "bulk"))
    question_count, candidates = candidate_ids.shape
    per_owner, feature_width = passages.shape
    pair_count = question_count * candidates
    capacity = 2 * pair_count // owners
    flat_ids = candidate_ids.reshape(pair_count)
    owner_of = flat_ids // per_owner
    row_of = flat_ids % per_owner
    member = (owner_of[:, None] == jnp.arange(owners, dtype=jnp.int32)[None, :]).astype(jnp.int32)
    earlier = jnp.cumsum(member, axis=0) - member
    send_slot = owner_of * capacity + jnp.sum(earlier * member, axis=1)
    request = jnp.zeros((owners * capacity,), jnp.int32).at[send_slot].set(row_of)
    log_reader = log_normalize(reader_loglik)
    reader_prob = jnp.exp(log_reader)
    wanted = send_requests(request)
    fetched = jnp.take(passages, wanted, axis=0)
    replies = return_rows(fetched)
    gathered = jnp.take(replies, send_slot, axis=0).reshape(
        question_count, candidates, feature_width
    )
    score_scale = 4.0 / math.sqrt(feature_width)
    scores = (
        jnp.einsum("qd,qkd->qk", questions, gathered, preferred_element_type=jnp.float32)
        * score_scale
    )
    log_retriever = log_normalize(scores)
    retriever_prob = jnp.exp(log_retriever)
    divergence = jnp.sum(reader_prob * (log_reader - log_retriever), axis=1)
    summed = lax.psum(jnp.sum(divergence), ("index", "bulk"))
    mean_divergence = summed / (question_count * owners)
    weights = (retriever_prob - reader_prob).astype(jnp.bfloat16)
    question_grads = (
        jnp.einsum("qk,qkd->qd", weights, gathered, preferred_element_type=jnp.float32)
        * score_scale
    )
    return (mean_divergence, question_grads)


def solution(mesh):
    placed = (
        P(("index", "bulk"), None),
        P(("index", "bulk"), None),
        P(("index", "bulk"), None),
        P(("index", "bulk"), None),
    )
    return jax.shard_map(
        body,
        mesh=mesh,
        in_specs=placed,
        out_specs=(P(), P(("index", "bulk"), None)),
        check_vma=False,
    )
```

profile of v0, /device:TPU:1, one launch (start us, length us, event | category | flops | bytes accessed | tf_op | source)
XLA Modules:
  0.0 169.3 jit_solution(14899278437184407410)
XLA Ops:
  0.6 0.9 reshape.198
  1.6 0.8 reshape.197
  2.4 0.8 reshape.200
  3.3 0.2 fusion.6
  3.5 0.8 copy-done.1
  4.3 1.1 broadcast_add_fusion
  5.5 0.4 fusion.5
  5.9 4.3 %scatter_custom_fusion = s32[2048]{0:T(1024)S(1)} fusion(s32[1024]{0:T(1024)S(1)} %bitcast.36, s32[1024]{0:T(1024)S(1)} %get-tuple-element.4, s32[]{:T(128)} %constant.64.clone.1), kind=kCustom, calls=%fused_computation.59 | custom fusion | bytes 8196 | tf_op jit(solution)/shard_map/scatter | solution.py:35
  10.3 21.1 %all_to_all.24 = s32[128,16,1]{1,2,0:T(1,128)S(1)} all-to-all(s32[128,16,1]{1,2,0:T(1,128)S(1)} %bitcast.30), channel_id=1, replica_groups=mesh['index'=8,'bulk'=16] {'index','bulk'}, dimensions={0} | all-to-all | bytes 16384 | tf_op jit(solution)/shard_map/all_to_all | solution.py:16
  31.5 0.5 broadcast.219
  32.0 0.8 reduce.4
  32.9 9.4 %gather_fusion = bf16[2048,768]{1,0:T(8,128)(2,1)} fusion(bf16[2048,768]{1,0:T(8,128)(2,1)S(1)} %copy-done, s32[2048]{0:T(1024)S(1)} %broadcast_clamp_fusion), kind=kCustom, calls=%fused_computation | custom fusion | bytes 6299648 | tf_op jit(solution)/shard_map/jit(_take)/gather | solution.py:39
  42.3 3.3 %broadcast_select_fusion = bf16[128,16,768]{2,1,0:T(8,128)(2,1)} fusion(bf16[128,16,768]{2,1,0:T(8,128)(2,1)} %bitcast.26, pred[128,16]{1,0:T(8,128)(4,1)S(1)} %compare_and_fusion), kind=kLoop, calls=%fused_computation.3 | loop fusion | flops 1572864 | bytes 6293504 | tf_op jit(solution)/shard_map/jit(_take)/select_n | solution.py:39
  45.7 5.4 %all-to-all-start.1 = ((bf16[128,16,768]{2,1,0:T(8,128)(2,1)}), bf16[128,16,768]{2,1,0:T(8,128)(2,1)}, u32[]{:S(2)}, u32[]{:S(2)}) async-start(bf16[128,16,768]{2,1,0:T(8,128)(2,1)} %broadcast_select_fusion), calls=%async_computation.1 | async-start | bytes 6291456 | tf_op jit(solution)/shard_map/all_to_all | solution.py:20
  51.2 0.2 exponential_reduce_fusion.1
  51.5 39.9 %all-to-all-done.1 = bf16[128,16,768]{2,1,0:T(8,128)(2,1)} async-done(((bf16[128,16,768]{2,1,0:T(8,128)(2,1)}), bf16[128,16,768]{2,1,0:T(8,128)(2,1)}, u32[]{:S(2)}, u32[]{:S(2)}) %all-to-all-start.1) | async-done | bytes 3145760 | tf_op jit(solution)/shard_map/all_to_all | solution.py:20
  91.4 7.9 %gather_fusion.1 = bf16[1024,768]{1,0:T(8,128)(2,1)} fusion(bf16[2048,768]{1,0:T(8,128)(2,1)} %bitcast.9, s32[1024]{0:T(1024)S(1)} %broadcast_clamp_fusion.1), kind=kCustom, calls=%fused_computation.1 | custom fusion | bytes 3149824 | tf_op jit(solution)/shard_map/jit(_take)/gather | solution.py:41
  99.3 2.1 %fusion.1 = f32[32,1,32]{2,1,0:T(1,128)S(1)} fusion(bf16[32,32,768]{2,1,0:T(8,128)(2,1)} %bitcast.27, pred[32,32]{1,0:T(8,128)(4,1)S(1)} %compare_and_fusion.1, bf16[32,768,1]{1,0,2:T(8,128)(2,1)S(1)} %bitcast.38), kind=kOutput, calls=%fused_computation.6 | convolution fusion | flops 2359296 | bytes 1627136 | tf_op jit(solution)/shard_map/qd,qkd->qk/dot_general | solution.py:46
  101.4 0.1 multiply_reduce_fusion.1
  101.5 0.2 exponential_reduce_fusion
  101.7 0.7 fusion.15
  102.4 0.4 fusion
  102.8 0.7 bitcast_multiply_fusion
  103.4 64.1 %psum.7 = f32[]{:T(128)} all-reduce(f32[]{:T(128)} %get-tuple-element.3), channel_id=1, replica_groups=mesh['index'=8,'bulk'=16] {'index','bulk'}, use_global_device_ids=true, to_apply=%region_9.10 | all-reduce | flops 1 | bytes 8 | tf_op jit(solution)/shard_map/psum | solution.py:52
  (30 shorter events, 0.7 us)
Async XLA Ops:
  0.6 32.3 %copy-start = (bf16[2048,768]{1,0:T(8,128)(2,1)S(1)}, bf16[2048,768]{1,0:T(8,128)(2,1)}, u32[]{:S(2)}) copy-start(bf16[2048,768]{1,0:T(8,128)(2,1)} %param.5) | copy-start | bytes 9437188
  3.5 0.8 copy-start.1
  45.7 5.4 %copy-start.4 = (f32[32,32]{1,0:T(8,128)S(1)}, f32[32,32]{1,0:T(8,128)}, u32[]{:S(2)}) copy-start(f32[32,32]{1,0:T(8,128)} %param.7) | copy-start | bytes 12292
  45.7 5.8 %copy-start.3 = (s32[32,32]{1,0:T(8,128)S(1)}, s32[32,32]{1,0:T(8,128)}, u32[]{:S(2)}) copy-start(s32[32,32]{1,0:T(8,128)} %param.6) | copy-start | bytes 12292
  45.7 45.7 %all-to-all-start.1 = ((bf16[128,16,768]{2,1,0:T(8,128)(2,1)}), bf16[128,16,768]{2,1,0:T(8,128)(2,1)}, u32[]{:S(2)}, u32[]{:S(2)}) async-start(bf16[128,16,768]{2,1,0:T(8,128)(2,1)} %broadcast_select_fusion), calls=%async_computation.1 | async-start | bytes 6291456 | tf_op jit(solution)/shard_map/all_to_all | solution.py:20
  91.4 7.9 %copy-start.5 = (bf16[32,768]{1,0:T(8,128)(2,1)S(1)}, bf16[32,768]{1,0:T(8,128)(2,1)}, u32[]{:S(2)}) copy-start(bf16[32,768]{1,0:T(8,128)(2,1)} %param.4) | copy-start | bytes 147460
  99.3 3.1 %copy-start.2 = (bf16[1024,768]{1,0:T(8,128)(2,1)S(1)}, bf16[1024,768]{1,0:T(8,128)(2,1)}, u32[]{:S(2)}) copy-start(bf16[1024,768]{1,0:T(8,128)(2,1)} %gather_fusion.1) | copy-start | bytes 4718596
where the time goes:
time: 170 us; the launch traced here: 169 us
  blocking collectives  85.2 us (50%)
  waiting for transfers between devices  39.9 us (23%)
  local copies, waits for them, and re-layouts  25.9 us (15%)
  other arithmetic  7.89 us (5%)
  starting transfers between devices  5.36 us (3%)
  between operations  2.59 us (2%)
  matrix products  2.5 us (1%)
    psum x1, blocking collectives, body(): summed = lax.psum(jnp.sum(divergence), ('index', 'bulk'))  64.1 us
    all_to_all x1, waiting for transfers between devices, return_rows(): lax.all_to_all(fetched, ('index', 'bulk'), split_axis=0, concat_axis=0, t...  39.9 us
    all_to_all x1, blocking collectives, send_requests(): lax.all_to_all(request, ('index', 'bulk'), split_axis=0, concat_axis=0, t...  21.1 us
    gather x1, local copies, waits for them, and re-layouts, body(): fetched = jnp.take(passages, wanted, axis=0)  9.38 us
    gather x1, local copies, waits for them, and re-layouts, body(): jnp.take(replies, send_slot, axis=0)  7.86 us
    all_to_all x1, starting transfers between devices, return_rows(): lax.all_to_all(fetched, ('index', 'bulk'), split_axis=0, concat_axis=0, t...  5.36 us
    scatter x1, local copies, waits for them, and re-layouts, body(): jnp.zeros((owners * capacity,), jnp.int32).at[send_slot].set(row_of)  4.32 us
  transfers between devices with their start and end apart: 1, of which 1 were waited for; matrix products, arithmetic and copies ran while one was open for 0% of the time, Pallas kernels for 0%

commit v1 on v0

v1 whole, which is shorter than its diff:
```python
import math

import jax
import jax.numpy as jnp
from jax import lax
from jax.experimental import pallas as pl
from jax.experimental.pallas import tpu as pltpu
from jax.sharding import PartitionSpec as P

AXES = ("index", "bulk")
LANES = 128
CAP = 16
VMEM = pl.BlockSpec(memory_space=pltpu.VMEM)


def exchange(blocks):
    return lax.all_to_all(blocks, AXES, split_axis=0, concat_axis=0, tiled=True)


def log_normalize(logits):
    highest = jnp.max(logits, axis=1, keepdims=True)
    shifted = logits - highest
    return shifted - jnp.log(jnp.sum(jnp.exp(shifted), axis=1, keepdims=True))


def as_lanes(ref):
    return jnp.concatenate([ref[pl.ds(b, 8, stride=4), :] for b in range(4)], axis=1)


def plan_kernel(ids_ref, reader_ref, request_ref, table_ref, reader_scratch):
    reader_scratch[...] = log_normalize(reader_ref[...])
    ids = as_lanes(ids_ref)
    log_reader = as_lanes(reader_scratch)
    owner = ids >> 11
    row = ids & 2047
    question = 4 * lax.broadcasted_iota(jnp.int32, (8, LANES), 0) + (
        lax.broadcasted_iota(jnp.int32, (8, LANES), 1) >> 5
    )
    high = (row >> 3).astype(jnp.float32)
    low = (((row & 7) << 5) | question).astype(jnp.float32)
    part0 = log_reader.astype(jnp.bfloat16).astype(jnp.float32)
    rest = log_reader - part0
    part1 = rest.astype(jnp.bfloat16).astype(jnp.float32)
    part2 = rest - part1
    owners = lax.broadcasted_iota(jnp.int32, (LANES, LANES), 0)
    member = [
        jnp.where(owner[a : a + 1, :] == owners, 1.0, 0.0).astype(jnp.float32) for a in range(8)
    ]
    member_low = [m.astype(jnp.bfloat16) for m in member]
    before = lax.broadcasted_iota(jnp.int32, (LANES, 2 * LANES), 0)
    after = lax.broadcasted_iota(jnp.int32, (LANES, 2 * LANES), 1)
    prefix = jnp.where((before < after) | (after >= LANES), 1.0, 0.0).astype(jnp.bfloat16)
    counts = jnp.dot(
        jnp.concatenate(member_low, axis=0), prefix, preferred_element_type=jnp.float32
    )
    slots = lax.broadcasted_iota(jnp.int32, (CAP, LANES), 0).astype(jnp.float32)
    carry = jnp.zeros((LANES, LANES), jnp.float32)
    left = []
    for a in range(8):
        block = counts[a * LANES : (a + 1) * LANES, :]
        rank = jnp.sum(member[a] * (block[:, :LANES] + carry), axis=0, keepdims=True)
        carry = carry + block[:, LANES:]
        here = jnp.where(slots == rank, 1.0, 0.0)
        values = [high, low, part0, part1, part2]
        pieces = [here * v[a : a + 1, :] for v in values] + [here]
        left.append(jnp.concatenate(pieces, axis=0).astype(jnp.bfloat16))
    table = lax.dot_general(
        jnp.concatenate(left, axis=1),
        jnp.concatenate(member_low, axis=1),
        (((1,), (1,)), ((), ())),
        preferred_element_type=jnp.float32,
    )
    table_ref[...] = table[CAP:, :]
    wanted = table[:CAP, :].astype(jnp.int32) * 8 + (table[CAP : 2 * CAP, :].astype(jnp.int32) >> 5)
    padded = jnp.concatenate([wanted, jnp.zeros((LANES - CAP, LANES), jnp.int32)], axis=0)
    request_ref[...] = padded.T


def slots_kernel(table_ref, info_ref):
    owners = lax.broadcasted_iota(jnp.int32, (LANES, LANES * CAP), 0)
    lanes = lax.broadcasted_iota(jnp.int32, (LANES, LANES * CAP), 1)
    spread = jnp.where((lanes >> 4) == owners, 1.0, 0.0).astype(jnp.bfloat16)
    wide = jnp.dot(
        table_ref[...].astype(jnp.bfloat16), spread, preferred_element_type=jnp.float32
    )
    own = (lanes[:CAP] & (CAP - 1)) == owners[:CAP]

    def pick(n):
        return jnp.sum(
            jnp.where(own, wide[n * CAP : (n + 1) * CAP, :], 0.0), axis=0, keepdims=True
        )

    question = pick(0).astype(jnp.int32) & 31
    question = jnp.where(pick(4) > 0.5, question, -1).astype(jnp.float32)
    log_reader = pick(1) + pick(2) + pick(3)
    info_ref[...] = jnp.concatenate(
        [question, log_reader, jnp.zeros((6, LANES * CAP), jnp.float32)], axis=0
    )


def fetch_kernel(wanted_ref, passages_ref, rows_ref, image, dense, index, sem):
    chunks = image.shape[0]
    total = jnp.zeros((CAP, LANES), jnp.int32)
    for k in range(8):
        part = wanted_ref[pl.ds(k, 16, stride=8), :]
        total = total + (pltpu.roll(part, CAP * k, 1) if k else part)
    dense[...] = total
    copy = pltpu.make_async_copy(dense, index, sem)
    copy.start()
    for c in range(chunks):
        image[c] = passages_ref[:, c * LANES : (c + 1) * LANES].astype(jnp.float32)
    copy.wait()
    sub = lax.broadcasted_iota(jnp.int32, (8, LANES), 0)

    def one_block(d, _):
        high = d >> 3
        low = (d & 7) * CAP
        halves = []
        for h in range(2):
            acc = None
            for j in range(8):
                r = index[high, low + h * 8 + j]
                got = [image[c, pl.ds(r, 8, stride=0), :] for c in range(chunks)]
                acc = got if acc is None else [jnp.where(sub == j, g, x) for g, x in zip(got, acc)]
            halves.append(acc)
        start = pl.multiple_of(d * CAP, CAP)
        for c in range(chunks):
            pair = jnp.concatenate([halves[0][c], halves[1][c]], axis=0).astype(jnp.bfloat16)
            rows_ref[pl.ds(start, CAP), c * LANES : (c + 1) * LANES] = pair
        return 0

    lax.fori_loop(0, LANES, one_block, 0)


def score_kernel(questions_ref, rows_ref, info_ref, grads_ref, part_ref):
    count, width = questions_ref.shape
    scale = 4.0 / math.sqrt(width)
    scores = (
        lax.dot_general(
            questions_ref[...],
            rows_ref[...],
            (((1,), (1,)), ((), ())),
            preferred_element_type=jnp.float32,
        )
        * scale
    )
    question = info_ref[0:1, :]
    log_reader = info_ref[1:2, :]
    mine = question == lax.broadcasted_iota(jnp.int32, scores.shape, 0).astype(jnp.float32)
    highest = jnp.max(jnp.where(mine, scores, -jnp.inf), axis=1, keepdims=True)
    shifted = jnp.where(mine, scores - highest, -jnp.inf)
    log_retriever = shifted - jnp.log(jnp.sum(jnp.exp(shifted), axis=1, keepdims=True))
    reader = jnp.exp(log_reader)
    weights = jnp.where(mine, jnp.exp(log_retriever) - reader, 0.0).astype(jnp.bfloat16)
    grads_ref[...] = (
        jnp.dot(weights, rows_ref[...], preferred_element_type=jnp.float32) * scale
    )
    own = jnp.sum(jnp.where(mine, log_retriever, 0.0), axis=0, keepdims=True)
    divergence = jnp.where(question >= 0.0, reader * (log_reader - own), 0.0)
    part_ref[...] = jnp.broadcast_to(jnp.sum(divergence, axis=1, keepdims=True), part_ref.shape)


def body(questions, passages, candidate_ids, reader_loglik):
    owners = lax.axis_size(AXES)
    question_count, width = questions.shape
    slot_count = owners * CAP
    request, table = pl.pallas_call(
        plan_kernel,
        out_shape=(
            jax.ShapeDtypeStruct((owners, LANES), jnp.int32),
            jax.ShapeDtypeStruct((5 * CAP, LANES), jnp.float32),
        ),
        in_specs=[VMEM, VMEM],
        out_specs=(VMEM, VMEM),
        scratch_shapes=[pltpu.VMEM(reader_loglik.shape, jnp.float32)],
        name="plan",
    )(candidate_ids, reader_loglik)
    wanted = exchange(request)
    info = pl.pallas_call(
        slots_kernel,
        out_shape=jax.ShapeDtypeStruct((8, slot_count), jnp.float32),
        in_specs=[VMEM],
        out_specs=VMEM,
        name="slots",
    )(table)
    fetched = pl.pallas_call(
        fetch_kernel,
        out_shape=jax.ShapeDtypeStruct((slot_count, width), passages.dtype),
        in_specs=[VMEM, VMEM],
        out_specs=VMEM,
        scratch_shapes=[
            pltpu.VMEM((width // LANES, passages.shape[0], LANES), jnp.float32),
            pltpu.VMEM((CAP, LANES), jnp.int32),
            pltpu.SMEM((CAP, LANES), jnp.int32),
            pltpu.SemaphoreType.DMA,
        ],
        name="fetch",
    )(wanted, passages)
    replies = exchange(fetched.reshape(owners, CAP, width)).reshape(slot_count, width)
    grads, part = pl.pallas_call(
        score_kernel,
        out_shape=(
            jax.ShapeDtypeStruct((question_count, width), jnp.float32),
            jax.ShapeDtypeStruct((owners, LANES), jnp.float32),
        ),
        in_specs=[VMEM, VMEM, VMEM],
        out_specs=(VMEM, VMEM),
        name="score",
    )(questions, replies, info)
    summed = jnp.sum(exchange(part), axis=0)[0]
    return (summed / (question_count * owners), grads)


def solution(mesh):
    placed = P(AXES, None)
    return jax.shard_map(
        body,
        mesh=mesh,
        in_specs=(placed, placed, placed, placed),
        out_specs=(P(), placed),
        check_vma=False,
    )
```

time: 170 us -> 104 us (0.61)
  blocking collectives: 85.2 us -> 36.2 us
  local copies, waits for them, and re-layouts: 25.9 us -> 1.65 us
  Pallas kernels: 0 us -> 20.7 us
  other arithmetic: 7.89 us -> 0.15 us
  matrix products: 2.5 us -> 0 us
    psum x1 -> x0, blocking collectives: 64.1 us -> none  [body(): summed = lax.psum(jnp.sum(divergence), ('index', 'bulk'))]
    pallas_call x0 -> x4, Pallas kernels: none -> 20.7 us  [the longest x1 12.4 us: body(): pl.pallas_call(fetch_kernel, out_shape=jax.ShapeDtypeStruct((slot_count,...]
    gather x2 -> x0, local copies, waits for them, and re-layouts: 17.2 us -> none  [the longest x1 9.38 us: body(): fetched = jnp.take(passages, wanted, axis=0)]
    all_to_all x1 -> x2, blocking collectives: 21.1 us -> 36.2 us  [exchange(): return lax.all_to_all(blocks, AXES, split_axis=0, concat_axis=0, tiled=True)]
    scatter x1 -> x0, local copies, waits for them, and re-layouts: 4.32 us -> none  [body(): jnp.zeros((owners * capacity,), jnp.int32).at[send_slot].set(row_of)]
    select_n x5 -> x0, other arithmetic: 3.4 us -> none  [the longest x2 3.35 us: body(): fetched = jnp.take(passages, wanted, axis=0)]
    reshape x3 -> x0, local copies, waits for them, and re-layouts: 2.54 us -> none  [body(): flat_ids = candidate_ids.reshape(pair_count)]
    dot_general x2 -> x0, matrix products: 2.5 us -> none  [the longest x1 2.11 us: body(): jnp.einsum('qd,qkd->qk', questions, gathered, preferred_element_type=jnp....]
  transfers between devices with their start and end apart: 1 -> 1, of which waited for: 1 -> 1; matrix products, arithmetic and copies ran while one was open for 0% -> 0% of each run, Pallas kernels for 0% -> 2%
where the time goes in v1:
time: 104 us
  waiting for transfers between devices  39 us (38%)
  blocking collectives  36.2 us (35%)
  Pallas kernels  20.7 us (20%)
  starting transfers between devices  4.28 us (4%)
  between operations  1.82 us (2%)
  local copies, waits for them, and re-layouts  1.65 us (2%)
    all_to_all x1, waiting for transfers between devices, exchange(): return lax.all_to_all(blocks, AXES, split_axis=0, concat_axis=0, tiled=True)  39 us
    all_to_all x2, blocking collectives, exchange(): return lax.all_to_all(blocks, AXES, split_axis=0, concat_axis=0, tiled=True)  36.2 us
    pallas_call x1, Pallas kernels, body(): pl.pallas_call(fetch_kernel, out_shape=jax.ShapeDtypeStruct((slot_count,...  12.4 us
    pallas_call x1, Pallas kernels, body(): pl.pallas_call(score_kernel, out_shape=(jax.ShapeDtypeStruct((question_co...  4.58 us
    all_to_all x1, starting transfers between devices, exchange(): return lax.all_to_all(blocks, AXES, split_axis=0, concat_axis=0, tiled=True)  4.28 us
  transfers between devices with their start and end apart: 1, of which 1 were waited for; matrix products, arithmetic and copies ran while one was open for 0% of the time, Pallas kernels for 2%

profile of v1, /device:TPU:1, one launch (start us, length us, event | category | flops | bytes accessed | tf_op | source)
XLA Modules:
  0.0 103.8 jit_solution(41418252055683526)
XLA Ops:
  0.6 2.1 %plan.1 = (s32[128,128]{1,0:T(8,128)}, f32[80,128]{1,0:T(8,128)}) custom-call(s32[32,32]{1,0:T(8,128)} %ids_ref.1, f32[32,32]{1,0:T(8,128)} %reader_ref.1), custom_call_target="tpu_custom_call" | custom-call | tf_op jit(solution)/shard_map/plan/pallas_call | solution.py:167
  2.7 21.6 %all_to_all.25 = s32[128,1,128]{2,1,0:T(1,128)} all-to-all(s32[128,1,128]{2,1,0:T(1,128)} %bitcast.15), channel_id=1, replica_groups=mesh['index'=8,'bulk'=16] {'index','bulk'}, dimensions={0} | all-to-all | bytes 131072 | tf_op jit(solution)/shard_map/all_to_all | solution.py:17
  24.3 12.4 %fetch.1 = bf16[2048,768]{1,0:T(8,128)(2,1)} custom-call(s32[128,128]{1,0:T(8,128)} %bitcast.13, bf16[2048,768]{1,0:T(8,128)(2,1)} %passages_ref.1), custom_call_target="tpu_custom_call" | custom-call | tf_op jit(solution)/shard_map/fetch/pallas_call | solution.py:186
  36.7 4.3 %all-to-all-start.1 = ((bf16[128,16,768]{2,1,0:T(8,128)(2,1)}), bf16[128,16,768]{2,1,0:T(8,128)(2,1)S(1)}, u32[]{:S(2)}, u32[]{:S(2)}) async-start(bf16[128,16,768]{2,1,0:T(8,128)(2,1)} %bitcast.12), calls=%async_computation.1 | async-start | bytes 6291456 | tf_op jit(solution)/shard_map/all_to_all | solution.py:17
  41.0 1.7 %slots.1.info_ref = f32[8,2048]{1,0:T(8,128)} custom-call(f32[80,128]{1,0:T(8,128)} %get-tuple-element.7.table_ref), custom_call_target="tpu_custom_call" | custom-call | tf_op jit(solution)/shard_map/slots/pallas_call | solution.py:179
  42.7 39.0 %all-to-all-done.1 = bf16[128,16,768]{2,1,0:T(8,128)(2,1)S(1)} async-done(((bf16[128,16,768]{2,1,0:T(8,128)(2,1)}), bf16[128,16,768]{2,1,0:T(8,128)(2,1)S(1)}, u32[]{:S(2)}, u32[]{:S(2)}) %all-to-all-start.1) | async-done | bytes 3145760 | tf_op jit(solution)/shard_map/all_to_all | solution.py:17
  81.6 0.0 copy-start
  81.6 1.6 %copy-done = bf16[128,16,768]{2,1,0:T(8,128)(2,1)} copy-done((bf16[128,16,768]{2,1,0:T(8,128)(2,1)}, bf16[128,16,768]{2,1,0:T(8,128)(2,1)S(1)}, u32[]{:S(2)}) %copy-start) | copy-done | bytes 3145752
  83.3 4.6 %score.1 = (f32[32,768]{1,0:T(8,128)}, f32[128,128]{1,0:T(8,128)}) custom-call(bf16[32,768]{1,0:T(8,128)(2,1)} %questions_ref.1, bf16[2048,768]{1,0:T(8,128)(2,1)} %bitcast.11, f32[8,2048]{1,0:T(8,128)} %slots.1.info_ref), custom_call_target="tpu_custom_call" | custom-call | tf_op jit(solution)/shard_map/score/pallas_call | solution.py:200
  87.9 14.7 %all_to_all.26 = f32[128,1,128]{2,1,0:T(1,128)S(1)} all-to-all(f32[128,1,128]{2,1,0:T(1,128)} %bitcast.14), channel_id=1, replica_groups=mesh['index'=8,'bulk'=16] {'index','bulk'}, dimensions={0} | all-to-all | bytes 131072 | tf_op jit(solution)/shard_map/all_to_all | solution.py:17
  102.5 0.2 reduce_sum.9
Async XLA Ops:
  36.7 44.9 %all-to-all-start.1 = ((bf16[128,16,768]{2,1,0:T(8,128)(2,1)}), bf16[128,16,768]{2,1,0:T(8,128)(2,1)S(1)}, u32[]{:S(2)}, u32[]{:S(2)}) async-start(bf16[128,16,768]{2,1,0:T(8,128)(2,1)} %bitcast.12), calls=%async_computation.1 | async-start | bytes 6291456 | tf_op jit(solution)/shard_map/all_to_all | solution.py:17
  81.6 1.7 %copy-start = (bf16[128,16,768]{2,1,0:T(8,128)(2,1)}, bf16[128,16,768]{2,1,0:T(8,128)(2,1)S(1)}, u32[]{:S(2)}) copy-start(bf16[128,16,768]{2,1,0:T(8,128)(2,1)S(1)} %all-to-all-done.1) | copy-start | bytes 9437188

commit v2 on v1

v2 whole, which is shorter than its diff:
```python
import math

import jax
import jax.numpy as jnp
from jax import lax
from jax.experimental import pallas as pl
from jax.experimental.pallas import tpu as pltpu
from jax.sharding import PartitionSpec as P

AXES = ("index", "bulk")
LANES = 128
CAP = 16
VMEM = pl.BlockSpec(memory_space=pltpu.VMEM)
HBM = pl.BlockSpec(memory_space=pltpu.HBM)
PARAMS = pltpu.CompilerParams(vmem_limit_bytes=24 << 20)


def in_vmem(array):
    return pltpu.with_memory_space_constraint(array, pltpu.VMEM)


def exchange(blocks):
    return lax.all_to_all(blocks, AXES, split_axis=0, concat_axis=0, tiled=True)


def log_normalize(logits):
    highest = jnp.max(logits, axis=1, keepdims=True)
    shifted = logits - highest
    return shifted - jnp.log(jnp.sum(jnp.exp(shifted), axis=1, keepdims=True))


def as_lanes(ref):
    return jnp.concatenate([ref[pl.ds(b, 8, stride=4), :] for b in range(4)], axis=1)


def members(owner):
    owners = lax.broadcasted_iota(jnp.int32, (LANES, LANES), 0)
    return [jnp.where(owner[a : a + 1, :] == owners, 1.0, 0.0) for a in range(8)]


def placements(member, values):
    member_low = [m.astype(jnp.bfloat16) for m in member]
    before = lax.broadcasted_iota(jnp.int32, (LANES, 2 * LANES), 0)
    after = lax.broadcasted_iota(jnp.int32, (LANES, 2 * LANES), 1)
    prefix = jnp.where((before < after) | (after >= LANES), 1.0, 0.0).astype(jnp.bfloat16)
    counts = jnp.dot(
        jnp.concatenate(member_low, axis=0), prefix, preferred_element_type=jnp.float32
    )
    slots = lax.broadcasted_iota(jnp.int32, (CAP, LANES), 0).astype(jnp.float32)
    carry = jnp.zeros((LANES, LANES), jnp.float32)
    left = []
    for a in range(8):
        block = counts[a * LANES : (a + 1) * LANES, :]
        rank = jnp.sum(member[a] * (block[:, :LANES] + carry), axis=0, keepdims=True)
        carry = carry + block[:, LANES:]
        here = jnp.where(slots == rank, 1.0, 0.0)
        pieces = [here if v is None else here * v[a : a + 1, :] for v in values]
        left.append(jnp.concatenate(pieces, axis=0).astype(jnp.bfloat16))
    return lax.dot_general(
        jnp.concatenate(left, axis=1),
        jnp.concatenate(member_low, axis=1),
        (((1,), (1,)), ((), ())),
        preferred_element_type=jnp.float32,
    )


def plan_kernel(ids_ref, passages_ref, request_ref, local_ref, sem):
    copy = pltpu.make_async_copy(passages_ref, local_ref, sem)
    copy.start()
    ids = as_lanes(ids_ref)
    row = ids & 2047
    high = (row >> 4).astype(jnp.float32)
    low = (row & 15).astype(jnp.float32)
    table = placements(members(ids >> 11), [high, low])
    wanted = (table[:CAP, :] * 16.0 + table[CAP:, :]).astype(jnp.int32)
    padded = jnp.concatenate([wanted, jnp.zeros((LANES - CAP, LANES), jnp.int32)], axis=0)
    request_ref[...] = padded.T
    copy.wait()


def slots_kernel(ids_ref, reader_ref, info_ref, reader_scratch):
    reader_scratch[...] = log_normalize(reader_ref[...])
    ids = as_lanes(ids_ref)
    log_reader = as_lanes(reader_scratch)
    question = 4 * lax.broadcasted_iota(jnp.int32, (8, LANES), 0) + (
        lax.broadcasted_iota(jnp.int32, (8, LANES), 1) >> 5
    )
    part0 = log_reader.astype(jnp.bfloat16).astype(jnp.float32)
    rest = log_reader - part0
    part1 = rest.astype(jnp.bfloat16).astype(jnp.float32)
    part2 = rest - part1
    table = placements(
        members(ids >> 11), [(question + 1).astype(jnp.float32), part0, part1, part2]
    )
    owners = lax.broadcasted_iota(jnp.int32, (LANES, LANES * CAP), 0)
    lanes = lax.broadcasted_iota(jnp.int32, (LANES, LANES * CAP), 1)
    spread = jnp.where((lanes >> 4) == owners, 1.0, 0.0).astype(jnp.bfloat16)
    wide = jnp.dot(table.astype(jnp.bfloat16), spread, preferred_element_type=jnp.float32)
    own = (lanes[:CAP] & (CAP - 1)) == owners[:CAP]

    def pick(n):
        return jnp.sum(
            jnp.where(own, wide[n * CAP : (n + 1) * CAP, :], 0.0), axis=0, keepdims=True
        )

    info_ref[...] = jnp.concatenate(
        [
            pick(0) - 1.0,
            pick(1) + pick(2) + pick(3),
            jnp.zeros((6, LANES * CAP), jnp.float32),
        ],
        axis=0,
    )


def fetch_kernel(wanted_ref, passages_ref, out_ref, image, rows, dense, index, sem, sends):
    chunks = image.shape[0]
    total = jnp.zeros((CAP, LANES), jnp.int32)
    for k in range(8):
        part = wanted_ref[pl.ds(k, 16, stride=8), :]
        total = total + (pltpu.roll(part, CAP * k, 1) if k else part)
    dense[...] = total
    copy = pltpu.make_async_copy(dense, index, sem)
    copy.start()
    for c in range(chunks):
        image[c, 8 : 8 + passages_ref.shape[0], :] = passages_ref[:, c * LANES : (c + 1) * LANES].astype(jnp.float32)
    copy.wait()
    sub = lax.broadcasted_iota(jnp.int32, (8, LANES), 0)

    def send(line):
        part = pl.ds(pl.multiple_of(line * LANES, LANES), LANES)
        return pltpu.make_async_copy(rows.at[part, :], out_ref.at[part, :], sends.at[line])

    def one_line(line, _):
        for d in range(8):
            halves = []
            for h in range(2):
                acc = None
                for j in range(8):
                    r = index[line, d * CAP + h * 8 + j]
                    got = [image[c, pl.ds(r + (8 - j), 8), :] for c in range(chunks)]
                    acc = (
                        got if acc is None else [jnp.where(sub == j, g, x) for g, x in zip(got, acc)]
                    )
                halves.append(acc)
            start = pl.multiple_of(line * LANES + d * CAP, CAP)
            for c in range(chunks):
                pair = jnp.concatenate([halves[0][c], halves[1][c]], axis=0).astype(jnp.bfloat16)
                rows[pl.ds(start, CAP), c * LANES : (c + 1) * LANES] = pair
        send(line).start()
        return 0

    lax.fori_loop(0, CAP, one_line, 0)
    for line in range(CAP):
        send(line).wait()


def score_kernel(questions_ref, rows_ref, info_ref, grads_ref, part_ref):
    count, width = questions_ref.shape
    scale = 4.0 / math.sqrt(width)
    scores = (
        lax.dot_general(
            questions_ref[...],
            rows_ref[...],
            (((1,), (1,)), ((), ())),
            preferred_element_type=jnp.float32,
        )
        * scale
    )
    question = info_ref[0:1, :]
    log_reader = info_ref[1:2, :]
    mine = question == lax.broadcasted_iota(jnp.int32, scores.shape, 0).astype(jnp.float32)
    highest = jnp.max(jnp.where(mine, scores, -jnp.inf), axis=1, keepdims=True)
    shifted = jnp.where(mine, scores - highest, -jnp.inf)
    log_retriever = shifted - jnp.log(jnp.sum(jnp.exp(shifted), axis=1, keepdims=True))
    reader = jnp.exp(log_reader)
    weights = jnp.where(mine, jnp.exp(log_retriever) - reader, 0.0).astype(jnp.bfloat16)
    grads_ref[...] = (
        jnp.dot(weights, rows_ref[...], preferred_element_type=jnp.float32) * scale
    )
    own = jnp.sum(jnp.where(mine, log_retriever, 0.0), axis=0, keepdims=True)
    divergence = jnp.where(question >= 0.0, reader * (log_reader - own), 0.0)
    total = jnp.sum(divergence, axis=1, keepdims=True) / (count * part_ref.shape[0])
    part_ref[...] = jnp.broadcast_to(total, part_ref.shape)


def body(questions, passages, candidate_ids, reader_loglik):
    owners = lax.axis_size(AXES)
    question_count, width = questions.shape
    slot_count = owners * CAP
    request, local = pl.pallas_call(
        plan_kernel,
        out_shape=(
            jax.ShapeDtypeStruct((owners, LANES), jnp.int32),
            pltpu.VMEM(passages.shape, passages.dtype),
        ),
        in_specs=[VMEM, HBM],
        out_specs=(VMEM, VMEM),
        scratch_shapes=[pltpu.SemaphoreType.DMA],
        compiler_params=PARAMS,
        name="plan",
    )(candidate_ids, pltpu.with_memory_space_constraint(passages, pltpu.HBM))
    wanted = exchange(request)
    info = pl.pallas_call(
        slots_kernel,
        out_shape=jax.ShapeDtypeStruct((8, slot_count), jnp.float32),
        in_specs=[VMEM, VMEM],
        out_specs=VMEM,
        scratch_shapes=[pltpu.VMEM(reader_loglik.shape, jnp.float32)],
        compiler_params=PARAMS,
        name="slots",
    )(candidate_ids, reader_loglik)
    fetched = pl.pallas_call(
        fetch_kernel,
        out_shape=pltpu.HBM((slot_count, width), passages.dtype),
        in_specs=[VMEM, VMEM],
        out_specs=HBM,
        scratch_shapes=[
            pltpu.VMEM((width // LANES, passages.shape[0] + CAP, LANES), jnp.float32),
            pltpu.VMEM((slot_count, width), passages.dtype),
            pltpu.VMEM((CAP, LANES), jnp.int32),
            pltpu.SMEM((CAP, LANES), jnp.int32),
            pltpu.SemaphoreType.DMA,
            pltpu.SemaphoreType.DMA((CAP,)),
        ],
        compiler_params=PARAMS,
        name="fetch",
    )(wanted, in_vmem(local))
    replies = exchange(fetched.reshape(owners, CAP, width)).reshape(slot_count, width)
    grads, part = pl.pallas_call(
        score_kernel,
        out_shape=(
            jax.ShapeDtypeStruct((question_count, width), jnp.float32),
            jax.ShapeDtypeStruct((owners, LANES), jnp.float32),
        ),
        in_specs=[VMEM, VMEM, VMEM],
        out_specs=(VMEM, VMEM),
        compiler_params=PARAMS,
        name="score",
    )(questions, in_vmem(replies), info)
    return (jnp.sum(exchange(part), axis=0)[0], grads)


def solution(mesh):
    placed = P(AXES, None)
    return jax.shard_map(
        body,
        mesh=mesh,
        in_specs=(placed, placed, placed, placed),
        out_specs=(P(), placed),
        check_vma=False,
    )
```

time: 104 us -> 92.6 us (0.89)
  Pallas kernels: 20.7 us -> 10.4 us
  between operations: 1.82 us -> 0.71 us
    pallas_call x1, Pallas kernels: 12.4 us -> 5.01 us  [body(): pl.pallas_call(fetch_kernel, out_shape=pltpu.HBM((slot_count, width), pas...]
    pallas_call x1, Pallas kernels: 4.58 us -> 2.69 us  [body(): pl.pallas_call(score_kernel, out_shape=(jax.ShapeDtypeStruct((question_co...]
  transfers between devices with their start and end apart: 1 -> 1, of which waited for: 1 -> 1; matrix products, arithmetic and copies ran while one was open for 0% -> 0% of each run, Pallas kernels for 2% -> 1%
where the time goes in v2:
time: 92.6 us; the launch traced here: 92.3 us
  waiting for transfers between devices  39.8 us (43%)
  blocking collectives  35.6 us (38%)
  Pallas kernels  10.4 us (11%)
  starting transfers between devices  4.39 us (5%)
    all_to_all x1, waiting for transfers between devices, exchange(): return lax.all_to_all(blocks, AXES, split_axis=0, concat_axis=0, tiled=True)  39.8 us
    all_to_all x2, blocking collectives, exchange(): return lax.all_to_all(blocks, AXES, split_axis=0, concat_axis=0, tiled=True)  35.6 us
    pallas_call x1, Pallas kernels, body(): pl.pallas_call(fetch_kernel, out_shape=pltpu.HBM((slot_count, width), pas...  5.01 us
    all_to_all x1, starting transfers between devices, exchange(): return lax.all_to_all(blocks, AXES, split_axis=0, concat_axis=0, tiled=True)  4.39 us
    pallas_call x1, Pallas kernels, body(): pl.pallas_call(score_kernel, out_shape=(jax.ShapeDtypeStruct((question_co...  2.69 us
    pallas_call x1, Pallas kernels, body(): pl.pallas_call(plan_kernel, out_shape=(jax.ShapeDtypeStruct((owners, LANE...  1.9 us
  transfers between devices with their start and end apart: 1, of which 1 were waited for; matrix products, arithmetic and copies ran while one was open for 0% of the time, Pallas kernels for 1%

profile of v2, /device:TPU:1, one launch (start us, length us, event | category | flops | bytes accessed | tf_op | source)
XLA Modules:
  0.0 92.3 jit_solution(4042933169704133525)
XLA Ops:
  0.6 0.0 copy-start
  0.6 0.7 copy-done
  1.4 1.9 %plan.1 = (s32[128,128]{1,0:T(8,128)S(1)}, bf16[2048,768]{1,0:T(8,128)(2,1)S(1)}) custom-call(s32[32,32]{1,0:T(8,128)S(1)} %copy-done, bf16[2048,768]{1,0:T(8,128)(2,1)} %passages_ref.1), custom_call_target="tpu_custom_call" | custom-call | tf_op jit(solution)/shard_map/plan/pallas_call | solution.py:191
  3.3 21.1 %all_to_all.25 = s32[128,1,128]{2,1,0:T(1,128)S(1)} all-to-all(s32[128,1,128]{2,1,0:T(1,128)S(1)} %bitcast.14), channel_id=1, replica_groups=mesh['index'=8,'bulk'=16] {'index','bulk'}, dimensions={0} | all-to-all | bytes 131072 | tf_op jit(solution)/shard_map/all_to_all | solution.py:23
  24.4 5.0 %fetch.1 = bf16[2048,768]{1,0:T(8,128)(2,1)} custom-call(s32[128,128]{1,0:T(8,128)S(1)} %bitcast.12, bf16[2048,768]{1,0:T(8,128)(2,1)S(1)} %get-tuple-element.7.passages_ref), custom_call_target="tpu_custom_call" | custom-call | tf_op jit(solution)/shard_map/fetch/pallas_call | solution.py:213
  29.4 0.0 copy-start.1
  29.4 0.0 copy-start.3
  29.4 0.0 copy-start.2
  29.4 4.4 %all-to-all-start.1 = ((bf16[128,16,768]{2,1,0:T(8,128)(2,1)}), bf16[128,16,768]{2,1,0:T(8,128)(2,1)S(1)}, u32[]{:S(2)}, u32[]{:S(2)}) async-start(bf16[128,16,768]{2,1,0:T(8,128)(2,1)} %bitcast.15), calls=%async_computation.1 | async-start | bytes 6291456 | tf_op jit(solution)/shard_map/all_to_all | solution.py:23
  33.8 0.0 copy-done.1
  33.8 0.0 copy-done.3
  33.8 0.9 slots.1.info_ref
  34.7 39.8 %all-to-all-done.1 = bf16[128,16,768]{2,1,0:T(8,128)(2,1)S(1)} async-done(((bf16[128,16,768]{2,1,0:T(8,128)(2,1)}), bf16[128,16,768]{2,1,0:T(8,128)(2,1)S(1)}, u32[]{:S(2)}, u32[]{:S(2)}) %all-to-all-start.1) | async-done | bytes 3145760 | tf_op jit(solution)/shard_map/all_to_all | solution.py:23
  74.5 0.0 copy-done.2
  74.5 2.7 %score.1 = (f32[32,768]{1,0:T(8,128)}, f32[128,128]{1,0:T(8,128)S(1)}) custom-call(bf16[32,768]{1,0:T(8,128)(2,1)S(1)} %copy-done.2, bf16[2048,768]{1,0:T(8,128)(2,1)S(1)} %bitcast.11, f32[8,2048]{1,0:T(8,128)S(1)} %slots.1.info_ref), custom_call_target="tpu_custom_call" | custom-call | tf_op jit(solution)/shard_map/score/pallas_call | solution.py:230
  77.2 14.5 %all_to_all.26 = f32[128,1,128]{2,1,0:T(1,128)S(1)} all-to-all(f32[128,1,128]{2,1,0:T(1,128)S(1)} %bitcast.13), channel_id=1, replica_groups=mesh['index'=8,'bulk'=16] {'index','bulk'}, dimensions={0} | all-to-all | bytes 131072 | tf_op jit(solution)/shard_map/all_to_all | solution.py:23
  91.6 0.7 reduce_sum.9
Async XLA Ops:
  0.6 0.7 copy-start
  29.4 4.4 %copy-start.1 = (s32[32,32]{1,0:T(8,128)S(1)}, s32[32,32]{1,0:T(8,128)}, u32[]{:S(2)}) copy-start(s32[32,32]{1,0:T(8,128)} %ids_ref.3) | copy-start | bytes 12292
  29.4 4.4 %copy-start.3 = (f32[32,32]{1,0:T(8,128)S(1)}, f32[32,32]{1,0:T(8,128)}, u32[]{:S(2)}) copy-start(f32[32,32]{1,0:T(8,128)} %reader_ref.1) | copy-start | bytes 12292
  29.4 45.1 %copy-start.2 = (bf16[32,768]{1,0:T(8,128)(2,1)S(1)}, bf16[32,768]{1,0:T(8,128)(2,1)}, u32[]{:S(2)}) copy-start(bf16[32,768]{1,0:T(8,128)(2,1)} %questions_ref.1) | copy-start | bytes 147460
  29.4 45.1 %all-to-all-start.1 = ((bf16[128,16,768]{2,1,0:T(8,128)(2,1)}), bf16[128,16,768]{2,1,0:T(8,128)(2,1)S(1)}, u32[]{:S(2)}, u32[]{:S(2)}) async-start(bf16[128,16,768]{2,1,0:T(8,128)(2,1)} %bitcast.15), calls=%async_computation.1 | async-start | bytes 6291456 | tf_op jit(solution)/shard_map/all_to_all | solution.py:23

commit v3 on v2

--- a/solution.py
+++ b/solution.py
@@ -64,9 +64,7 @@
     )
 
 
-def plan_kernel(ids_ref, passages_ref, request_ref, local_ref, sem):
-    copy = pltpu.make_async_copy(passages_ref, local_ref, sem)
-    copy.start()
+def plan_kernel(ids_ref, request_ref):
     ids = as_lanes(ids_ref)
     row = ids & 2047
     high = (row >> 4).astype(jnp.float32)
@@ -75,6 +73,11 @@
     wanted = (table[:CAP, :] * 16.0 + table[CAP:, :]).astype(jnp.int32)
     padded = jnp.concatenate([wanted, jnp.zeros((LANES - CAP, LANES), jnp.int32)], axis=0)
     request_ref[...] = padded.T
+
+
+def load_kernel(passages_ref, local_ref, sem):
+    copy = pltpu.make_async_copy(passages_ref, local_ref, sem)
+    copy.start()
     copy.wait()
 
 
@@ -123,7 +126,9 @@
     copy = pltpu.make_async_copy(dense, index, sem)
     copy.start()
     for c in range(chunks):
-        image[c, 8 : 8 + passages_ref.shape[0], :] = passages_ref[:, c * LANES : (c + 1) * LANES].astype(jnp.float32)
+        image[c, 8 : 8 + passages_ref.shape[0], :] = passages_ref[
+            :, c * LANES : (c + 1) * LANES
+        ].astype(jnp.float32)
     copy.wait()
     sub = lax.broadcasted_iota(jnp.int32, (8, LANES), 0)
 
@@ -155,7 +160,7 @@
         send(line).wait()
 
 
-def score_kernel(questions_ref, rows_ref, info_ref, grads_ref, part_ref):
+def score_kernel(questions_ref, rows_ref, info_ref, weights_ref, part_ref):
     count, width = questions_ref.shape
     scale = 4.0 / math.sqrt(width)
     scores = (
@@ -174,36 +179,45 @@
     shifted = jnp.where(mine, scores - highest, -jnp.inf)
     log_retriever = shifted - jnp.log(jnp.sum(jnp.exp(shifted), axis=1, keepdims=True))
     reader = jnp.exp(log_reader)
-    weights = jnp.where(mine, jnp.exp(log_retriever) - reader, 0.0).astype(jnp.bfloat16)
-    grads_ref[...] = (
-        jnp.dot(weights, rows_ref[...], preferred_element_type=jnp.float32) * scale
-    )
+    weights_ref[...] = jnp.where(mine, jnp.exp(log_retriever) - reader, 0.0).astype(jnp.bfloat16)
     own = jnp.sum(jnp.where(mine, log_retriever, 0.0), axis=0, keepdims=True)
     divergence = jnp.where(question >= 0.0, reader * (log_reader - own), 0.0)
     total = jnp.sum(divergence, axis=1, keepdims=True) / (count * part_ref.shape[0])
     part_ref[...] = jnp.broadcast_to(total, part_ref.shape)
 
 
+def grads_kernel(weights_ref, rows_ref, grads_ref):
+    scale = 4.0 / math.sqrt(rows_ref.shape[1])
+    grads_ref[...] = (
+        jnp.dot(weights_ref[...], rows_ref[...], preferred_element_type=jnp.float32) * scale
+    )
+
+
 def body(questions, passages, candidate_ids, reader_loglik):
     owners = lax.axis_size(AXES)
     question_count, width = questions.shape
     slot_count = owners * CAP
-    request, local = pl.pallas_call(
+    request = pl.pallas_call(
         plan_kernel,
-        out_shape=(
-            jax.ShapeDtypeStruct((owners, LANES), jnp.int32),
-            pltpu.VMEM(passages.shape, passages.dtype),
-        ),
-        in_specs=[VMEM, HBM],
-        out_specs=(VMEM, VMEM),
+        out_shape=pltpu.VMEM((owners, LANES), jnp.int32),
+        in_specs=[VMEM],
+        out_specs=VMEM,
+        compiler_params=PARAMS,
+        name="plan",
+    )(candidate_ids)
+    wanted = exchange(request)
+    local = pl.pallas_call(
+        load_kernel,
+        out_shape=pltpu.VMEM(passages.shape, passages.dtype),
+        in_specs=[HBM],
+        out_specs=VMEM,
         scratch_shapes=[pltpu.SemaphoreType.DMA],
         compiler_params=PARAMS,
-        name="plan",
-    )(candidate_ids, pltpu.with_memory_space_constraint(passages, pltpu.HBM))
-    wanted = exchange(request)
+        name="load",
+    )(pltpu.with_memory_space_constraint(passages, pltpu.HBM))
     info = pl.pallas_call(
         slots_kernel,
-        out_shape=jax.ShapeDtypeStruct((8, slot_count), jnp.float32),
+        out_shape=pltpu.VMEM((8, slot_count), jnp.float32),
         in_specs=[VMEM, VMEM],
         out_specs=VMEM,
         scratch_shapes=[pltpu.VMEM(reader_loglik.shape, jnp.float32)],
@@ -227,18 +241,28 @@
         name="fetch",
     )(wanted, in_vmem(local))
     replies = exchange(fetched.reshape(owners, CAP, width)).reshape(slot_count, width)
-    grads, part = pl.pallas_call(
+    replies = in_vmem(replies)
+    weights, part = pl.pallas_call(
         score_kernel,
         out_shape=(
-            jax.ShapeDtypeStruct((question_count, width), jnp.float32),
-            jax.ShapeDtypeStruct((owners, LANES), jnp.float32),
+            pltpu.VMEM((question_count, slot_count), jnp.bfloat16),
+            pltpu.VMEM((owners, LANES), jnp.float32),
         ),
         in_specs=[VMEM, VMEM, VMEM],
         out_specs=(VMEM, VMEM),
         compiler_params=PARAMS,
         name="score",
-    )(questions, in_vmem(replies), info)
-    return (jnp.sum(exchange(part), axis=0)[0], grads)
+    )(questions, replies, info)
+    summed = exchange(part)
+    grads = pl.pallas_call(
+        grads_kernel,
+        out_shape=jax.ShapeDtypeStruct((question_count, width), jnp.float32),
+        in_specs=[VMEM, VMEM],
+        out_specs=VMEM,
+        compiler_params=PARAMS,
+        name="grads",
+    )(weights, replies)
+    return (jnp.sum(summed, axis=0)[0], grads)
 
 
 def solution(mesh):

time: 92.6 us -> 91.7 us (level)
  blocking collectives: 35.6 us -> 0 us
  starting transfers between devices: 4.39 us -> 20.7 us
  waiting for transfers between devices: 39.8 us -> 56.1 us
  Pallas kernels: 10.4 us -> 12.4 us
    all_to_all x2 -> x0, blocking collectives: 35.6 us -> none  [exchange(): return lax.all_to_all(blocks, AXES, split_axis=0, concat_axis=0, tiled=True)]
    all_to_all x1 -> x3, waiting for transfers between devices: 39.8 us -> 56.1 us  [exchange(): return lax.all_to_all(blocks, AXES, split_axis=0, concat_axis=0, tiled=True)]
    all_to_all x1 -> x3, starting transfers between devices: 4.39 us -> 20.7 us  [exchange(): return lax.all_to_all(blocks, AXES, split_axis=0, concat_axis=0, tiled=True)]
    pallas_call x3 -> x5, Pallas kernels: 5.44 us -> 7.39 us  [the longest x1 2.04 us: body(): pl.pallas_call(score_kernel, out_shape=(pltpu.VMEM((question_count, slot_...]
  transfers between devices with their start and end apart: 1 -> 3, of which waited for: 1 -> 3; matrix products, arithmetic and copies ran while one was open for 0% -> 0% of each run, Pallas kernels for 1% -> 4%
where the time goes in v3:
time: 91.7 us; the launch traced here: 91.4 us
  waiting for transfers between devices  56.1 us (61%)
  starting transfers between devices  20.7 us (23%)
  Pallas kernels  12.4 us (14%)
    all_to_all x3, waiting for transfers between devices, exchange(): return lax.all_to_all(blocks, AXES, split_axis=0, concat_axis=0, tiled=True)  56.1 us
    all_to_all x3, starting transfers between devices, exchange(): return lax.all_to_all(blocks, AXES, split_axis=0, concat_axis=0, tiled=True)  20.7 us
    pallas_call x1, Pallas kernels, body(): pl.pallas_call(fetch_kernel, out_shape=pltpu.HBM((slot_count, width), pas...  5.02 us
    pallas_call x1, Pallas kernels, body(): pl.pallas_call(score_kernel, out_shape=(pltpu.VMEM((question_count, slot_...  2.04 us
    pallas_call x1, Pallas kernels, body(): pl.pallas_call(load_kernel, out_shape=pltpu.VMEM(passages.shape, passages...  1.9 us
  transfers between devices with their start and end apart: 3, of which 3 were waited for; matrix products, arithmetic and copies ran while one was open for 0% of the time, Pallas kernels for 4%

profile of v3, /device:TPU:1, one launch (start us, length us, event | category | flops | bytes accessed | tf_op | source)
XLA Modules:
  0.0 91.4 jit_solution(434177408256746555)
XLA Ops:
  0.6 0.0 copy-start
  0.6 0.7 copy-done
  1.3 1.3 %plan.1 = s32[128,128]{1,0:T(8,128)} custom-call(s32[32,32]{1,0:T(8,128)S(1)} %copy-done), custom_call_target="tpu_custom_call" | custom-call | tf_op jit(solution)/shard_map/plan/pallas_call | solution.py:200
  2.7 11.5 %all-to-all-start = ((s32[128,1,128]{2,1,0:T(1,128)}), s32[128,1,128]{2,1,0:T(1,128)S(1)}, u32[]{:S(2)}, u32[]{:S(2)}) async-start(s32[128,1,128]{2,1,0:T(1,128)} %bitcast.1), calls=%async_computation | async-start | bytes 131072 | tf_op jit(solution)/shard_map/all_to_all | solution.py:23
  14.2 1.9 %load.1.passages_ref = bf16[2048,768]{1,0:T(8,128)(2,1)S(1)} custom-call(bf16[2048,768]{1,0:T(8,128)(2,1)} %passages_ref.1), custom_call_target="tpu_custom_call" | custom-call | tf_op jit(solution)/shard_map/load/pallas_call | solution.py:209
  16.1 7.8 %all-to-all-done = s32[128,1,128]{2,1,0:T(1,128)S(1)} async-done(((s32[128,1,128]{2,1,0:T(1,128)}), s32[128,1,128]{2,1,0:T(1,128)S(1)}, u32[]{:S(2)}, u32[]{:S(2)}) %all-to-all-start) | async-done | bytes 65568 | tf_op jit(solution)/shard_map/all_to_all | solution.py:23
  23.9 5.0 %fetch.1 = bf16[2048,768]{1,0:T(8,128)(2,1)} custom-call(s32[128,128]{1,0:T(8,128)S(1)} %bitcast.13, bf16[2048,768]{1,0:T(8,128)(2,1)S(1)} %load.1.passages_ref), custom_call_target="tpu_custom_call" | custom-call | tf_op jit(solution)/shard_map/fetch/pallas_call | solution.py:227
  28.9 0.0 copy-start.1
  28.9 0.0 copy-start.3
  28.9 0.0 copy-start.2
  28.9 4.4 %all-to-all-start.1 = ((bf16[128,16,768]{2,1,0:T(8,128)(2,1)}), bf16[128,16,768]{2,1,0:T(8,128)(2,1)S(1)}, u32[]{:S(2)}, u32[]{:S(2)}) async-start(bf16[128,16,768]{2,1,0:T(8,128)(2,1)} %bitcast.14), calls=%async_computation.1 | async-start | bytes 6291456 | tf_op jit(solution)/shard_map/all_to_all | solution.py:23
  33.3 0.0 copy-done.1
  33.3 0.0 copy-done.3
  33.3 0.9 slots.1.info_ref
  34.2 39.8 %all-to-all-done.1 = bf16[128,16,768]{2,1,0:T(8,128)(2,1)S(1)} async-done(((bf16[128,16,768]{2,1,0:T(8,128)(2,1)}), bf16[128,16,768]{2,1,0:T(8,128)(2,1)S(1)}, u32[]{:S(2)}, u32[]{:S(2)}) %all-to-all-start.1) | async-done | bytes 3145760 | tf_op jit(solution)/shard_map/all_to_all | solution.py:23
  74.0 0.0 copy-done.2
  74.0 2.0 %score.1 = (bf16[32,2048]{1,0:T(8,128)(2,1)S(1)}, f32[128,128]{1,0:T(8,128)}) custom-call(bf16[32,768]{1,0:T(8,128)(2,1)S(1)} %copy-done.2, bf16[2048,768]{1,0:T(8,128)(2,1)S(1)} %bitcast.11, f32[8,2048]{1,0:T(8,128)S(1)} %slots.1.info_ref), custom_call_target="tpu_custom_call" | custom-call | tf_op jit(solution)/shard_map/score/pallas_call | solution.py:245
  76.0 4.9 %all-to-all-start.2 = ((f32[128,1,128]{2,1,0:T(1,128)}), f32[128,1,128]{2,1,0:T(1,128)S(1)}, u32[]{:S(2)}, u32[]{:S(2)}) async-start(f32[128,1,128]{2,1,0:T(1,128)} %bitcast.6), calls=%async_computation.2 | async-start | bytes 131072 | tf_op jit(solution)/shard_map/all_to_all | solution.py:23
  80.9 1.3 %grads.1 = f32[32,768]{1,0:T(8,128)} custom-call(bf16[32,2048]{1,0:T(8,128)(2,1)S(1)} %get-tuple-element.5.weights_ref, bf16[2048,768]{1,0:T(8,128)(2,1)S(1)} %bitcast.12), custom_call_target="tpu_custom_call" | custom-call | tf_op jit(solution)/shard_map/grads/pallas_call | solution.py:257
  82.2 8.5 %all-to-all-done.2 = f32[128,1,128]{2,1,0:T(1,128)S(1)} async-done(((f32[128,1,128]{2,1,0:T(1,128)}), f32[128,1,128]{2,1,0:T(1,128)S(1)}, u32[]{:S(2)}, u32[]{:S(2)}) %all-to-all-start.2) | async-done | bytes 65568 | tf_op jit(solution)/shard_map/all_to_all | solution.py:23
  90.7 0.7 reduce_sum.9
Async XLA Ops:
  0.6 0.7 copy-start
  2.7 21.2 %all-to-all-start = ((s32[128,1,128]{2,1,0:T(1,128)}), s32[128,1,128]{2,1,0:T(1,128)S(1)}, u32[]{:S(2)}, u32[]{:S(2)}) async-start(s32[128,1,128]{2,1,0:T(1,128)} %bitcast.1), calls=%async_computation | async-start | bytes 131072 | tf_op jit(solution)/shard_map/all_to_all | solution.py:23
  28.9 4.4 %copy-start.1 = (s32[32,32]{1,0:T(8,128)S(1)}, s32[32,32]{1,0:T(8,128)}, u32[]{:S(2)}) copy-start(s32[32,32]{1,0:T(8,128)} %ids_ref.3) | copy-start | bytes 12292
  28.9 4.4 %copy-start.3 = (f32[32,32]{1,0:T(8,128)S(1)}, f32[32,32]{1,0:T(8,128)}, u32[]{:S(2)}) copy-start(f32[32,32]{1,0:T(8,128)} %reader_ref.1) | copy-start | bytes 12292
  28.9 45.1 %copy-start.2 = (bf16[32,768]{1,0:T(8,128)(2,1)S(1)}, bf16[32,768]{1,0:T(8,128)(2,1)}, u32[]{:S(2)}) copy-start(bf16[32,768]{1,0:T(8,128)(2,1)} %questions_ref.1) | copy-start | bytes 147460
  28.9 45.0 %all-to-all-start.1 = ((bf16[128,16,768]{2,1,0:T(8,128)(2,1)}), bf16[128,16,768]{2,1,0:T(8,128)(2,1)S(1)}, u32[]{:S(2)}, u32[]{:S(2)}) async-start(bf16[128,16,768]{2,1,0:T(8,128)(2,1)} %bitcast.14), calls=%async_computation.1 | async-start | bytes 6291456 | tf_op jit(solution)/shard_map/all_to_all | solution.py:23
  76.0 14.7 %all-to-all-start.2 = ((f32[128,1,128]{2,1,0:T(1,128)}), f32[128,1,128]{2,1,0:T(1,128)S(1)}, u32[]{:S(2)}, u32[]{:S(2)}) async-start(f32[128,1,128]{2,1,0:T(1,128)} %bitcast.6), calls=%async_computation.2 | async-start | bytes 131072 | tf_op jit(solution)/shard_map/all_to_all | solution.py:23

commit v4 on v3

--- a/solution.py
+++ b/solution.py
@@ -17,6 +17,10 @@
 
 def in_vmem(array):
     return pltpu.with_memory_space_constraint(array, pltpu.VMEM)
+
+
+def in_hbm(array):
+    return pltpu.with_memory_space_constraint(array, pltpu.HBM)
 
 
 def exchange(blocks):
@@ -75,14 +79,16 @@
     request_ref[...] = padded.T
 
 
-def load_kernel(passages_ref, local_ref, sem):
-    copy = pltpu.make_async_copy(passages_ref, local_ref, sem)
-    copy.start()
-    copy.wait()
-
-
-def slots_kernel(ids_ref, reader_ref, info_ref, reader_scratch):
-    reader_scratch[...] = log_normalize(reader_ref[...])
+def prepare_kernel(
+    ids_hbm, reader_hbm, passages_ref, info_ref, local_ref, ids_ref, reader_scratch, sems
+):
+    pairs = ((reader_hbm, reader_scratch), (ids_hbm, ids_ref), (passages_ref, local_ref))
+    copies = [pltpu.make_async_copy(a, b, sems.at[n]) for n, (a, b) in enumerate(pairs)]
+    for copy in copies:
+        copy.start()
+    copies[0].wait()
+    reader_scratch[...] = log_normalize(reader_scratch[...])
+    copies[1].wait()
     ids = as_lanes(ids_ref)
     log_reader = as_lanes(reader_scratch)
     question = 4 * lax.broadcasted_iota(jnp.int32, (8, LANES), 0) + (
@@ -114,9 +120,10 @@
         ],
         axis=0,
     )
-
-
-def fetch_kernel(wanted_ref, passages_ref, out_ref, image, rows, dense, index, sem, sends):
+    copies[2].wait()
+
+
+def fetch_kernel(wanted_ref, passages_ref, rows, image, dense, index, sem):
     chunks = image.shape[0]
     total = jnp.zeros((CAP, LANES), jnp.int32)
     for k in range(8):
@@ -131,10 +138,6 @@
         ].astype(jnp.float32)
     copy.wait()
     sub = lax.broadcasted_iota(jnp.int32, (8, LANES), 0)
-
-    def send(line):
-        part = pl.ds(pl.multiple_of(line * LANES, LANES), LANES)
-        return pltpu.make_async_copy(rows.at[part, :], out_ref.at[part, :], sends.at[line])
 
     def one_line(line, _):
         for d in range(8):
@@ -152,12 +155,9 @@
             for c in range(chunks):
                 pair = jnp.concatenate([halves[0][c], halves[1][c]], axis=0).astype(jnp.bfloat16)
                 rows[pl.ds(start, CAP), c * LANES : (c + 1) * LANES] = pair
-        send(line).start()
         return 0
 
     lax.fori_loop(0, CAP, one_line, 0)
-    for line in range(CAP):
-        send(line).wait()
 
 
 def score_kernel(questions_ref, rows_ref, info_ref, weights_ref, part_ref):
@@ -206,36 +206,32 @@
         name="plan",
     )(candidate_ids)
     wanted = exchange(request)
-    local = pl.pallas_call(
-        load_kernel,
-        out_shape=pltpu.VMEM(passages.shape, passages.dtype),
-        in_specs=[HBM],
-        out_specs=VMEM,
-        scratch_shapes=[pltpu.SemaphoreType.DMA],
-        compiler_params=PARAMS,
-        name="load",
-    )(pltpu.with_memory_space_constraint(passages, pltpu.HBM))
-    info = pl.pallas_call(
-        slots_kernel,
-        out_shape=pltpu.VMEM((8, slot_count), jnp.float32),
+    info, local = pl.pallas_call(
+        prepare_kernel,
+        out_shape=(
+            pltpu.VMEM((8, slot_count), jnp.float32),
+            pltpu.VMEM(passages.shape, passages.dtype),
+        ),
+        in_specs=[HBM, HBM, HBM],
+        out_specs=(VMEM, VMEM),
+        scratch_shapes=[
+            pltpu.VMEM(candidate_ids.shape, jnp.int32),
+            pltpu.VMEM(reader_loglik.shape, jnp.float32),
+            pltpu.SemaphoreType.DMA((3,)),
+        ],
+        compiler_params=PARAMS,
+        name="prepare",
+    )(in_hbm(candidate_ids), in_hbm(reader_loglik), in_hbm(passages))
+    fetched = pl.pallas_call(
+        fetch_kernel,
+        out_shape=pltpu.VMEM((slot_count, width), passages.dtype),
         in_specs=[VMEM, VMEM],
         out_specs=VMEM,
-        scratch_shapes=[pltpu.VMEM(reader_loglik.shape, jnp.float32)],
-        compiler_params=PARAMS,
-        name="slots",
-    )(candidate_ids, reader_loglik)
-    fetched = pl.pallas_call(
-        fetch_kernel,
-        out_shape=pltpu.HBM((slot_count, width), passages.dtype),
-        in_specs=[VMEM, VMEM],
-        out_specs=HBM,
         scratch_shapes=[
             pltpu.VMEM((width // LANES, passages.shape[0] + CAP, LANES), jnp.float32),
-            pltpu.VMEM((slot_count, width), passages.dtype),
             pltpu.VMEM((CAP, LANES), jnp.int32),
             pltpu.SMEM((CAP, LANES), jnp.int32),
             pltpu.SemaphoreType.DMA,
-            pltpu.SemaphoreType.DMA((CAP,)),
         ],
         compiler_params=PARAMS,
         name="fetch",

time: 91.7 us -> 90.4 us (0.986)
  blocking collectives: 0 us -> 44.6 us
  waiting for transfers between devices: 56.1 us -> 16.3 us
  starting transfers between devices: 20.7 us -> 16.3 us
  Pallas kernels: 12.4 us -> 10.8 us
    all_to_all x0 -> x1, blocking collectives: none -> 44.6 us  [exchange(): return lax.all_to_all(blocks, AXES, split_axis=0, concat_axis=0, tiled=True)]
    all_to_all x3 -> x2, waiting for transfers between devices: 56.1 us -> 16.3 us  [exchange(): return lax.all_to_all(blocks, AXES, split_axis=0, concat_axis=0, tiled=True)]
    all_to_all x3 -> x2, starting transfers between devices: 20.7 us -> 16.3 us  [exchange(): return lax.all_to_all(blocks, AXES, split_axis=0, concat_axis=0, tiled=True)]
    pallas_call x3 -> x2, Pallas kernels: 7.77 us -> 6.16 us  [the longest x1 4.21 us: body(): pl.pallas_call(fetch_kernel, out_shape=pltpu.VMEM((slot_count, width), pa...]
  transfers between devices with their start and end apart: 3 -> 2, of which waited for: 3 -> 2; matrix products, arithmetic and copies ran while one was open for 0% -> 0% of each run, Pallas kernels for 4% -> 4%
where the time goes in v4:
time: 90.4 us; the launch traced here: 90 us
  blocking collectives  44.6 us (49%)
  starting transfers between devices  16.3 us (18%)
  waiting for transfers between devices  16.3 us (18%)
  Pallas kernels  10.8 us (12%)
    all_to_all x1, blocking collectives, exchange(): return lax.all_to_all(blocks, AXES, split_axis=0, concat_axis=0, tiled=True)  44.6 us
    all_to_all x2, starting transfers between devices, exchange(): return lax.all_to_all(blocks, AXES, split_axis=0, concat_axis=0, tiled=True)  16.3 us
    all_to_all x2, waiting for transfers between devices, exchange(): return lax.all_to_all(blocks, AXES, split_axis=0, concat_axis=0, tiled=True)  16.3 us
    pallas_call x1, Pallas kernels, body(): pl.pallas_call(fetch_kernel, out_shape=pltpu.VMEM((slot_count, width), pa...  4.21 us
    pallas_call x1, Pallas kernels, body(): pl.pallas_call(score_kernel, out_shape=(pltpu.VMEM((question_count, slot_...  2.03 us
    pallas_call x1, Pallas kernels, body(): pl.pallas_call(prepare_kernel, out_shape=(pltpu.VMEM((8, slot_count), jnp...  1.95 us
  transfers between devices with their start and end apart: 2, of which 2 were waited for; matrix products, arithmetic and copies ran while one was open for 0% of the time, Pallas kernels for 4%

profile of v4, /device:TPU:1, one launch (start us, length us, event | category | flops | bytes accessed | tf_op | source)
XLA Modules:
  0.0 90.0 jit_solution(4028755871704719202)
XLA Ops:
  0.6 0.0 copy-start
  0.6 0.7 copy-done
  1.3 1.3 %plan.1 = s32[128,128]{1,0:T(8,128)} custom-call(s32[32,32]{1,0:T(8,128)S(1)} %copy-done), custom_call_target="tpu_custom_call" | custom-call | tf_op jit(solution)/shard_map/plan/pallas_call | solution.py:200
  2.7 11.5 %all-to-all-start = ((s32[128,1,128]{2,1,0:T(1,128)}), s32[128,1,128]{2,1,0:T(1,128)S(1)}, u32[]{:S(2)}, u32[]{:S(2)}) async-start(s32[128,1,128]{2,1,0:T(1,128)} %bitcast.1), calls=%async_computation | async-start | bytes 131072 | tf_op jit(solution)/shard_map/all_to_all | solution.py:27
  14.2 2.0 %prepare.1 = (f32[8,2048]{1,0:T(8,128)S(1)}, bf16[2048,768]{1,0:T(8,128)(2,1)S(1)}) custom-call(s32[32,32]{1,0:T(8,128)} %ids_hbm.1, f32[32,32]{1,0:T(8,128)} %reader_hbm.1, bf16[2048,768]{1,0:T(8,128)(2,1)} %passages_ref.1), custom_call_target="tpu_custom_call" | custom-call | tf_op jit(solution)/shard_map/prepare/pallas_call | solution.py:209
  16.1 7.8 %all-to-all-done = s32[128,1,128]{2,1,0:T(1,128)S(1)} async-done(((s32[128,1,128]{2,1,0:T(1,128)}), s32[128,1,128]{2,1,0:T(1,128)S(1)}, u32[]{:S(2)}, u32[]{:S(2)}) %all-to-all-start) | async-done | bytes 65568 | tf_op jit(solution)/shard_map/all_to_all | solution.py:27
  23.9 4.2 %fetch.1 = bf16[2048,768]{1,0:T(8,128)(2,1)S(1)} custom-call(s32[128,128]{1,0:T(8,128)S(1)} %bitcast.14, bf16[2048,768]{1,0:T(8,128)(2,1)S(1)} %get-tuple-element.6.passages_ref), custom_call_target="tpu_custom_call" | custom-call | tf_op jit(solution)/shard_map/fetch/pallas_call | solution.py:225
  28.1 0.0 copy-start.1
  28.1 44.6 %all_to_all.25 = bf16[128,16,768]{2,1,0:T(8,128)(2,1)S(1)} all-to-all(bf16[128,16,768]{2,1,0:T(8,128)(2,1)S(1)} %bitcast.13), channel_id=1, replica_groups=mesh['index'=8,'bulk'=16] {'index','bulk'}, dimensions={0} | all-to-all | bytes 6291456 | tf_op jit(solution)/shard_map/all_to_all | solution.py:27
  72.7 0.0 copy-done.1
  72.7 2.0 %score.1 = (bf16[32,2048]{1,0:T(8,128)(2,1)S(1)}, f32[128,128]{1,0:T(8,128)}) custom-call(bf16[32,768]{1,0:T(8,128)(2,1)S(1)} %copy-done.1, bf16[2048,768]{1,0:T(8,128)(2,1)S(1)} %bitcast.11, f32[8,2048]{1,0:T(8,128)S(1)} %get-tuple-element.7.info_ref), custom_call_target="tpu_custom_call" | custom-call | tf_op jit(solution)/shard_map/score/pallas_call | solution.py:241
  74.7 4.9 %all-to-all-start.2 = ((f32[128,1,128]{2,1,0:T(1,128)}), f32[128,1,128]{2,1,0:T(1,128)S(1)}, u32[]{:S(2)}, u32[]{:S(2)}) async-start(f32[128,1,128]{2,1,0:T(1,128)} %bitcast.6), calls=%async_computation.2 | async-start | bytes 131072 | tf_op jit(solution)/shard_map/all_to_all | solution.py:27
  79.6 1.3 %grads.1 = f32[32,768]{1,0:T(8,128)} custom-call(bf16[32,2048]{1,0:T(8,128)(2,1)S(1)} %get-tuple-element.9.weights_ref, bf16[2048,768]{1,0:T(8,128)(2,1)S(1)} %bitcast.12), custom_call_target="tpu_custom_call" | custom-call | tf_op jit(solution)/shard_map/grads/pallas_call | solution.py:253
  80.9 8.5 %all-to-all-done.2 = f32[128,1,128]{2,1,0:T(1,128)S(1)} async-done(((f32[128,1,128]{2,1,0:T(1,128)}), f32[128,1,128]{2,1,0:T(1,128)S(1)}, u32[]{:S(2)}, u32[]{:S(2)}) %all-to-all-start.2) | async-done | bytes 65568 | tf_op jit(solution)/shard_map/all_to_all | solution.py:27
  89.4 0.7 reduce_sum.9
Async XLA Ops:
  0.6 0.7 copy-start
  2.7 21.2 %all-to-all-start = ((s32[128,1,128]{2,1,0:T(1,128)}), s32[128,1,128]{2,1,0:T(1,128)S(1)}, u32[]{:S(2)}, u32[]{:S(2)}) async-start(s32[128,1,128]{2,1,0:T(1,128)} %bitcast.1), calls=%async_computation | async-start | bytes 131072 | tf_op jit(solution)/shard_map/all_to_all | solution.py:27
  28.1 44.6 %copy-start.1 = (bf16[32,768]{1,0:T(8,128)(2,1)S(1)}, bf16[32,768]{1,0:T(8,128)(2,1)}, u32[]{:S(2)}) copy-start(bf16[32,768]{1,0:T(8,128)(2,1)} %questions_ref.1) | copy-start | bytes 147460
  74.7 14.7 %all-to-all-start.2 = ((f32[128,1,128]{2,1,0:T(1,128)}), f32[128,1,128]{2,1,0:T(1,128)S(1)}, u32[]{:S(2)}, u32[]{:S(2)}) async-start(f32[128,1,128]{2,1,0:T(1,128)} %bitcast.6), calls=%async_computation.2 | async-start | bytes 131072 | tf_op jit(solution)/shard_map/all_to_all | solution.py:27

commit v5 on v4

--- a/solution.py
+++ b/solution.py
@@ -10,6 +10,8 @@
 AXES = ("index", "bulk")
 LANES = 128
 CAP = 16
+STRIDE = 2048 + 4
+STEP = LANES + 4
 VMEM = pl.BlockSpec(memory_space=pltpu.VMEM)
 HBM = pl.BlockSpec(memory_space=pltpu.HBM)
 PARAMS = pltpu.CompilerParams(vmem_limit_bytes=24 << 20)
@@ -123,8 +125,9 @@
     copies[2].wait()
 
 
-def fetch_kernel(wanted_ref, passages_ref, rows, image, dense, index, sem):
-    chunks = image.shape[0]
+def fetch_kernel(wanted_ref, passages_ref, rows_ref, image, even, odd, dense, index, sem):
+    count, width = passages_ref.shape
+    chunks = width // LANES
     total = jnp.zeros((CAP, LANES), jnp.int32)
     for k in range(8):
         part = wanted_ref[pl.ds(k, 16, stride=8), :]
@@ -133,34 +136,31 @@
     copy = pltpu.make_async_copy(dense, index, sem)
     copy.start()
     for c in range(chunks):
-        image[c, 8 : 8 + passages_ref.shape[0], :] = passages_ref[
+        image[c * STRIDE : c * STRIDE + count, :] = passages_ref[
             :, c * LANES : (c + 1) * LANES
         ].astype(jnp.float32)
     copy.wait()
-    sub = lax.broadcasted_iota(jnp.int32, (8, LANES), 0)
-
-    def one_line(line, _):
-        for d in range(8):
-            halves = []
-            for h in range(2):
-                acc = None
-                for j in range(8):
-                    r = index[line, d * CAP + h * 8 + j]
-                    got = [image[c, pl.ds(r + (8 - j), 8), :] for c in range(chunks)]
-                    acc = (
-                        got if acc is None else [jnp.where(sub == j, g, x) for g, x in zip(got, acc)]
-                    )
-                halves.append(acc)
-            start = pl.multiple_of(line * LANES + d * CAP, CAP)
-            for c in range(chunks):
-                pair = jnp.concatenate([halves[0][c], halves[1][c]], axis=0).astype(jnp.bfloat16)
-                rows[pl.ds(start, CAP), c * LANES : (c + 1) * LANES] = pair
-        return 0
-
-    lax.fori_loop(0, CAP, one_line, 0)
-
-
-def score_kernel(questions_ref, rows_ref, info_ref, weights_ref, part_ref):
+
+    def move(line, moved):
+        for k in range(LANES):
+            r = index[line, k]
+            moved[pl.ds(k, chunks, stride=STEP), :] = image[pl.ds(r, chunks, stride=STRIDE), :]
+
+    def pack(line, moved):
+        for c in range(chunks):
+            rows_ref[line * LANES : (line + 1) * LANES, c * LANES : (c + 1) * LANES] = moved[
+                c * STEP : c * STEP + LANES, :
+            ].astype(rows_ref.dtype)
+
+    buffers = (even, odd)
+    move(0, even)
+    for line in range(1, CAP):
+        move(line, buffers[line % 2])
+        pack(line - 1, buffers[(line - 1) % 2])
+    pack(CAP - 1, odd)
+
+
+def score_kernel(questions_ref, rows_ref, info_ref, logs_ref, part_ref):
     count, width = questions_ref.shape
     scale = 4.0 / math.sqrt(width)
     scores = (
@@ -179,18 +179,21 @@
     shifted = jnp.where(mine, scores - highest, -jnp.inf)
     log_retriever = shifted - jnp.log(jnp.sum(jnp.exp(shifted), axis=1, keepdims=True))
     reader = jnp.exp(log_reader)
-    weights_ref[...] = jnp.where(mine, jnp.exp(log_retriever) - reader, 0.0).astype(jnp.bfloat16)
+    logs_ref[...] = log_retriever
     own = jnp.sum(jnp.where(mine, log_retriever, 0.0), axis=0, keepdims=True)
     divergence = jnp.where(question >= 0.0, reader * (log_reader - own), 0.0)
     total = jnp.sum(divergence, axis=1, keepdims=True) / (count * part_ref.shape[0])
     part_ref[...] = jnp.broadcast_to(total, part_ref.shape)
 
 
-def grads_kernel(weights_ref, rows_ref, grads_ref):
+def grads_kernel(logs_ref, info_ref, rows_ref, grads_ref):
     scale = 4.0 / math.sqrt(rows_ref.shape[1])
-    grads_ref[...] = (
-        jnp.dot(weights_ref[...], rows_ref[...], preferred_element_type=jnp.float32) * scale
-    )
+    mine = info_ref[0:1, :] == lax.broadcasted_iota(jnp.int32, logs_ref.shape, 0).astype(
+        jnp.float32
+    )
+    gap = jnp.exp(logs_ref[...]) - jnp.exp(info_ref[1:2, :])
+    weights = jnp.where(mine, gap, 0.0).astype(jnp.bfloat16)
+    grads_ref[...] = jnp.dot(weights, rows_ref[...], preferred_element_type=jnp.float32) * scale
 
 
 def body(questions, passages, candidate_ids, reader_loglik):
@@ -228,7 +231,9 @@
         in_specs=[VMEM, VMEM],
         out_specs=VMEM,
         scratch_shapes=[
-            pltpu.VMEM((width // LANES, passages.shape[0] + CAP, LANES), jnp.float32),
+            pltpu.VMEM((width // LANES * STRIDE, LANES), jnp.float32),
+            pltpu.VMEM((width // LANES * STEP, LANES), jnp.float32),
+            pltpu.VMEM((width // LANES * STEP, LANES), jnp.float32),
             pltpu.VMEM((CAP, LANES), jnp.int32),
             pltpu.SMEM((CAP, LANES), jnp.int32),
             pltpu.SemaphoreType.DMA,
@@ -238,10 +243,10 @@
     )(wanted, in_vmem(local))
     replies = exchange(fetched.reshape(owners, CAP, width)).reshape(slot_count, width)
     replies = in_vmem(replies)
-    weights, part = pl.pallas_call(
+    logs, part = pl.pallas_call(
         score_kernel,
         out_shape=(
-            pltpu.VMEM((question_count, slot_count), jnp.bfloat16),
+            pltpu.VMEM((question_count, slot_count), jnp.float32),
             pltpu.VMEM((owners, LANES), jnp.float32),
         ),
         in_specs=[VMEM, VMEM, VMEM],
@@ -253,11 +258,11 @@
     grads = pl.pallas_call(
         grads_kernel,
         out_shape=jax.ShapeDtypeStruct((question_count, width), jnp.float32),
-        in_specs=[VMEM, VMEM],
+        in_specs=[VMEM, VMEM, VMEM],
         out_specs=VMEM,
         compiler_params=PARAMS,
         name="grads",
-    )(weights, replies)
+    )(logs, info, replies)
     return (jnp.sum(summed, axis=0)[0], grads)
 
 

time: 90.4 us -> 89 us (0.985)
  Pallas kernels: 10.8 us -> 9.31 us
    pallas_call x1, Pallas kernels: 4.21 us -> 2.81 us  [body(): pl.pallas_call(fetch_kernel, out_shape=pltpu.VMEM((slot_count, width), pa...]
where the time goes in v5:
time: 89 us; the launch traced here: 88.6 us
  blocking collectives  44.6 us (50%)
  starting transfers between devices  16.3 us (18%)
  waiting for transfers between devices  16.3 us (18%)
  Pallas kernels  9.31 us (10%)
    all_to_all x1, blocking collectives, exchange(): return lax.all_to_all(blocks, AXES, split_axis=0, concat_axis=0, tiled=True)  44.6 us
    all_to_all x2, starting transfers between devices, exchange(): return lax.all_to_all(blocks, AXES, split_axis=0, concat_axis=0, tiled=True)  16.3 us
    all_to_all x2, waiting for transfers between devices, exchange(): return lax.all_to_all(blocks, AXES, split_axis=0, concat_axis=0, tiled=True)  16.3 us
    pallas_call x1, Pallas kernels, body(): pl.pallas_call(fetch_kernel, out_shape=pltpu.VMEM((slot_count, width), pa...  2.81 us
    pallas_call x1, Pallas kernels, body(): pl.pallas_call(score_kernel, out_shape=(pltpu.VMEM((question_count, slot_...  1.99 us
    pallas_call x1, Pallas kernels, body(): pl.pallas_call(prepare_kernel, out_shape=(pltpu.VMEM((8, slot_count), jnp...  1.95 us
  transfers between devices with their start and end apart: 2, of which 2 were waited for; matrix products, arithmetic and copies ran while one was open for 0% of the time, Pallas kernels for 4%

profile of v5, /device:TPU:1, one launch (start us, length us, event | category | flops | bytes accessed | tf_op | source)
XLA Modules:
  0.0 88.6 jit_solution(17031974783121844001)
XLA Ops:
  0.6 0.0 copy-start
  0.6 0.7 copy-done
  1.3 1.3 %plan.1 = s32[128,128]{1,0:T(8,128)} custom-call(s32[32,32]{1,0:T(8,128)S(1)} %copy-done), custom_call_target="tpu_custom_call" | custom-call | tf_op jit(solution)/shard_map/plan/pallas_call | solution.py:203
  2.7 11.5 %all-to-all-start = ((s32[128,1,128]{2,1,0:T(1,128)}), s32[128,1,128]{2,1,0:T(1,128)S(1)}, u32[]{:S(2)}, u32[]{:S(2)}) async-start(s32[128,1,128]{2,1,0:T(1,128)} %bitcast.1), calls=%async_computation | async-start | bytes 131072 | tf_op jit(solution)/shard_map/all_to_all | solution.py:29
  14.2 2.0 %prepare.1 = (f32[8,2048]{1,0:T(8,128)S(1)}, bf16[2048,768]{1,0:T(8,128)(2,1)S(1)}) custom-call(s32[32,32]{1,0:T(8,128)} %ids_hbm.1, f32[32,32]{1,0:T(8,128)} %reader_hbm.1, bf16[2048,768]{1,0:T(8,128)(2,1)} %passages_ref.1), custom_call_target="tpu_custom_call" | custom-call | tf_op jit(solution)/shard_map/prepare/pallas_call | solution.py:212
  16.1 7.8 %all-to-all-done = s32[128,1,128]{2,1,0:T(1,128)S(1)} async-done(((s32[128,1,128]{2,1,0:T(1,128)}), s32[128,1,128]{2,1,0:T(1,128)S(1)}, u32[]{:S(2)}, u32[]{:S(2)}) %all-to-all-start) | async-done | bytes 65568 | tf_op jit(solution)/shard_map/all_to_all | solution.py:29
  23.9 2.8 %fetch.1 = bf16[2048,768]{1,0:T(8,128)(2,1)S(1)} custom-call(s32[128,128]{1,0:T(8,128)S(1)} %bitcast.14, bf16[2048,768]{1,0:T(8,128)(2,1)S(1)} %get-tuple-element.6.passages_ref), custom_call_target="tpu_custom_call" | custom-call | tf_op jit(solution)/shard_map/fetch/pallas_call | solution.py:228
  26.7 0.0 copy-start.1
  26.7 44.6 %all_to_all.25 = bf16[128,16,768]{2,1,0:T(8,128)(2,1)S(1)} all-to-all(bf16[128,16,768]{2,1,0:T(8,128)(2,1)S(1)} %bitcast.13), channel_id=1, replica_groups=mesh['index'=8,'bulk'=16] {'index','bulk'}, dimensions={0} | all-to-all | bytes 6291456 | tf_op jit(solution)/shard_map/all_to_all | solution.py:29
  71.3 0.0 copy-done.1
  71.3 2.0 %score.1 = (f32[32,2048]{1,0:T(8,128)S(1)}, f32[128,128]{1,0:T(8,128)}) custom-call(bf16[32,768]{1,0:T(8,128)(2,1)S(1)} %copy-done.1, bf16[2048,768]{1,0:T(8,128)(2,1)S(1)} %bitcast.11, f32[8,2048]{1,0:T(8,128)S(1)} %get-tuple-element.7.info_ref), custom_call_target="tpu_custom_call" | custom-call | tf_op jit(solution)/shard_map/score/pallas_call | solution.py:246
  73.3 4.9 %all-to-all-start.2 = ((f32[128,1,128]{2,1,0:T(1,128)}), f32[128,1,128]{2,1,0:T(1,128)S(1)}, u32[]{:S(2)}, u32[]{:S(2)}) async-start(f32[128,1,128]{2,1,0:T(1,128)} %bitcast.6), calls=%async_computation.2 | async-start | bytes 131072 | tf_op jit(solution)/shard_map/all_to_all | solution.py:29
  78.2 1.3 %grads.1 = f32[32,768]{1,0:T(8,128)} custom-call(f32[32,2048]{1,0:T(8,128)S(1)} %get-tuple-element.9.logs_ref, f32[8,2048]{1,0:T(8,128)S(1)} %get-tuple-element.7.info_ref, bf16[2048,768]{1,0:T(8,128)(2,1)S(1)} %bitcast.12), custom_call_target="tpu_custom_call" | custom-call | tf_op jit(solution)/shard_map/grads/pallas_call | solution.py:258
  79.4 8.5 %all-to-all-done.2 = f32[128,1,128]{2,1,0:T(1,128)S(1)} async-done(((f32[128,1,128]{2,1,0:T(1,128)}), f32[128,1,128]{2,1,0:T(1,128)S(1)}, u32[]{:S(2)}, u32[]{:S(2)}) %all-to-all-start.2) | async-done | bytes 65568 | tf_op jit(solution)/shard_map/all_to_all | solution.py:29
  88.0 0.7 reduce_sum.9
Async XLA Ops:
  0.6 0.7 copy-start
  2.7 21.2 %all-to-all-start = ((s32[128,1,128]{2,1,0:T(1,128)}), s32[128,1,128]{2,1,0:T(1,128)S(1)}, u32[]{:S(2)}, u32[]{:S(2)}) async-start(s32[128,1,128]{2,1,0:T(1,128)} %bitcast.1), calls=%async_computation | async-start | bytes 131072 | tf_op jit(solution)/shard_map/all_to_all | solution.py:29
  26.7 44.6 %copy-start.1 = (bf16[32,768]{1,0:T(8,128)(2,1)S(1)}, bf16[32,768]{1,0:T(8,128)(2,1)}, u32[]{:S(2)}) copy-start(bf16[32,768]{1,0:T(8,128)(2,1)} %questions_ref.1) | copy-start | bytes 147460
  73.3 14.7 %all-to-all-start.2 = ((f32[128,1,128]{2,1,0:T(1,128)}), f32[128,1,128]{2,1,0:T(1,128)S(1)}, u32[]{:S(2)}, u32[]{:S(2)}) async-start(f32[128,1,128]{2,1,0:T(1,128)} %bitcast.6), calls=%async_computation.2 | async-start | bytes 131072 | tf_op jit(solution)/shard_map/all_to_all | solution.py:29

commit v6 on v5

--- a/solution.py
+++ b/solution.py
@@ -45,26 +45,23 @@
 
 
 def placements(member, values):
-    member_low = [m.astype(jnp.bfloat16) for m in member]
-    before = lax.broadcasted_iota(jnp.int32, (LANES, 2 * LANES), 0)
-    after = lax.broadcasted_iota(jnp.int32, (LANES, 2 * LANES), 1)
-    prefix = jnp.where((before < after) | (after >= LANES), 1.0, 0.0).astype(jnp.bfloat16)
-    counts = jnp.dot(
-        jnp.concatenate(member_low, axis=0), prefix, preferred_element_type=jnp.float32
-    )
-    slots = lax.broadcasted_iota(jnp.int32, (CAP, LANES), 0).astype(jnp.float32)
-    carry = jnp.zeros((LANES, LANES), jnp.float32)
+    before = lax.broadcasted_iota(jnp.int32, (LANES, LANES), 0)
+    after = lax.broadcasted_iota(jnp.int32, (LANES, LANES), 1)
+    prefix = jnp.where(before < after, 1.0, 0.0).astype(jnp.bfloat16)
+    above = [jnp.zeros((LANES, LANES), jnp.float32)]
+    for m in member:
+        above.append(above[-1] + m)
+    left_of = jnp.dot(above[8].astype(jnp.bfloat16), prefix, preferred_element_type=jnp.float32)
+    places = lax.broadcasted_iota(jnp.int32, (CAP, LANES), 0).astype(jnp.float32)
     left = []
     for a in range(8):
-        block = counts[a * LANES : (a + 1) * LANES, :]
-        rank = jnp.sum(member[a] * (block[:, :LANES] + carry), axis=0, keepdims=True)
-        carry = carry + block[:, LANES:]
-        here = jnp.where(slots == rank, 1.0, 0.0)
-        pieces = [here if v is None else here * v[a : a + 1, :] for v in values]
+        place = jnp.sum(member[a] * (left_of + above[a]), axis=0, keepdims=True)
+        here = jnp.where(places == place, 1.0, 0.0)
+        pieces = [here * v[a : a + 1, :] for v in values]
         left.append(jnp.concatenate(pieces, axis=0).astype(jnp.bfloat16))
     return lax.dot_general(
         jnp.concatenate(left, axis=1),
-        jnp.concatenate(member_low, axis=1),
+        jnp.concatenate([m.astype(jnp.bfloat16) for m in member], axis=1),
         (((1,), (1,)), ((), ())),
         preferred_element_type=jnp.float32,
     )
@@ -93,7 +90,7 @@
     copies[1].wait()
     ids = as_lanes(ids_ref)
     log_reader = as_lanes(reader_scratch)
-    question = 4 * lax.broadcasted_iota(jnp.int32, (8, LANES), 0) + (
+    number = 4 * lax.broadcasted_iota(jnp.int32, (8, LANES), 0) + (
         lax.broadcasted_iota(jnp.int32, (8, LANES), 1) >> 5
     )
     part0 = log_reader.astype(jnp.bfloat16).astype(jnp.float32)
@@ -101,7 +98,7 @@
     part1 = rest.astype(jnp.bfloat16).astype(jnp.float32)
     part2 = rest - part1
     table = placements(
-        members(ids >> 11), [(question + 1).astype(jnp.float32), part0, part1, part2]
+        members(ids >> 11), [(number + 1).astype(jnp.float32), part0, part1, part2]
     )
     owners = lax.broadcasted_iota(jnp.int32, (LANES, LANES * CAP), 0)
     lanes = lax.broadcasted_iota(jnp.int32, (LANES, LANES * CAP), 1)
@@ -114,14 +111,11 @@
             jnp.where(own, wide[n * CAP : (n + 1) * CAP, :], 0.0), axis=0, keepdims=True
         )
 
-    info_ref[...] = jnp.concatenate(
-        [
-            pick(0) - 1.0,
-            pick(1) + pick(2) + pick(3),
-            jnp.zeros((6, LANES * CAP), jnp.float32),
-        ],
-        axis=0,
-    )
+    question = pick(0) - 1.0
+    log_reader = pick(1) + pick(2) + pick(3)
+    reader = jnp.where(question >= 0.0, jnp.exp(log_reader), 0.0)
+    rest = jnp.zeros((5, LANES * CAP), jnp.float32)
+    info_ref[...] = jnp.concatenate([question, log_reader, reader, rest], axis=0)
     copies[2].wait()
 
 
@@ -172,17 +166,18 @@
         )
         * scale
     )
-    question = info_ref[0:1, :]
     log_reader = info_ref[1:2, :]
-    mine = question == lax.broadcasted_iota(jnp.int32, scores.shape, 0).astype(jnp.float32)
-    highest = jnp.max(jnp.where(mine, scores, -jnp.inf), axis=1, keepdims=True)
-    shifted = jnp.where(mine, scores - highest, -jnp.inf)
-    log_retriever = shifted - jnp.log(jnp.sum(jnp.exp(shifted), axis=1, keepdims=True))
-    reader = jnp.exp(log_reader)
-    logs_ref[...] = log_retriever
-    own = jnp.sum(jnp.where(mine, log_retriever, 0.0), axis=0, keepdims=True)
-    divergence = jnp.where(question >= 0.0, reader * (log_reader - own), 0.0)
-    total = jnp.sum(divergence, axis=1, keepdims=True) / (count * part_ref.shape[0])
+    reader = info_ref[2:3, :]
+    mine = info_ref[0:1, :] == lax.broadcasted_iota(jnp.int32, scores.shape, 0).astype(jnp.float32)
+    masked = jnp.where(mine, scores, -jnp.inf)
+    shifted = masked - jnp.max(masked, axis=1, keepdims=True)
+    own = jnp.sum(jnp.where(mine, shifted, 0.0), axis=0, keepdims=True)
+    known = jnp.sum(reader * (log_reader - own), axis=1, keepdims=True)
+    mass = jnp.sum(jnp.where(mine, reader, 0.0), axis=1, keepdims=True)
+    log_total = jnp.log(jnp.sum(jnp.exp(shifted), axis=1, keepdims=True))
+    logs_ref[...] = shifted - log_total
+    divergence = known + jnp.sum(mass * log_total, axis=0, keepdims=True)
+    total = divergence / (count * part_ref.shape[0])
     part_ref[...] = jnp.broadcast_to(total, part_ref.shape)
 
 
@@ -191,7 +186,7 @@
     mine = info_ref[0:1, :] == lax.broadcasted_iota(jnp.int32, logs_ref.shape, 0).astype(
         jnp.float32
     )
-    gap = jnp.exp(logs_ref[...]) - jnp.exp(info_ref[1:2, :])
+    gap = jnp.exp(logs_ref[...]) - info_ref[2:3, :]
     weights = jnp.where(mine, gap, 0.0).astype(jnp.bfloat16)
     grads_ref[...] = jnp.dot(weights, rows_ref[...], preferred_element_type=jnp.float32) * scale
 

time: 89 us -> 88.7 us (level)
  no operation moved by 1% of the time
where the time goes in v6:
time: 88.7 us; the launch traced here: 88.4 us
  blocking collectives  44.6 us (50%)
  starting transfers between devices  16.3 us (18%)
  waiting for transfers between devices  16.3 us (18%)
  Pallas kernels  9.1 us (10%)
    all_to_all x1, blocking collectives, exchange(): return lax.all_to_all(blocks, AXES, split_axis=0, concat_axis=0, tiled=True)  44.6 us
    all_to_all x2, starting transfers between devices, exchange(): return lax.all_to_all(blocks, AXES, split_axis=0, concat_axis=0, tiled=True)  16.3 us
    all_to_all x2, waiting for transfers between devices, exchange(): return lax.all_to_all(blocks, AXES, split_axis=0, concat_axis=0, tiled=True)  16.3 us
    pallas_call x1, Pallas kernels, body(): pl.pallas_call(fetch_kernel, out_shape=pltpu.VMEM((slot_count, width), pa...  2.81 us
    pallas_call x1, Pallas kernels, body(): pl.pallas_call(prepare_kernel, out_shape=(pltpu.VMEM((8, slot_count), jnp...  1.95 us
    pallas_call x1, Pallas kernels, body(): pl.pallas_call(score_kernel, out_shape=(pltpu.VMEM((question_count, slot_...  1.89 us
  transfers between devices with their start and end apart: 2, of which 2 were waited for; matrix products, arithmetic and copies ran while one was open for 0% of the time, Pallas kernels for 4%

profile of v6, /device:TPU:1, one launch (start us, length us, event | category | flops | bytes accessed | tf_op | source)
XLA Modules:
  0.0 88.4 jit_solution(1534632787668987874)
XLA Ops:
  0.6 0.0 copy-start
  0.6 0.7 copy-done
  1.3 1.2 %plan.1 = s32[128,128]{1,0:T(8,128)} custom-call(s32[32,32]{1,0:T(8,128)S(1)} %copy-done), custom_call_target="tpu_custom_call" | custom-call | tf_op jit(solution)/shard_map/plan/pallas_call | solution.py:198
  2.5 11.5 %all-to-all-start = ((s32[128,1,128]{2,1,0:T(1,128)}), s32[128,1,128]{2,1,0:T(1,128)S(1)}, u32[]{:S(2)}, u32[]{:S(2)}) async-start(s32[128,1,128]{2,1,0:T(1,128)} %bitcast.1), calls=%async_computation | async-start | bytes 131072 | tf_op jit(solution)/shard_map/all_to_all | solution.py:29
  14.0 2.0 %prepare.1 = (f32[8,2048]{1,0:T(8,128)S(1)}, bf16[2048,768]{1,0:T(8,128)(2,1)S(1)}) custom-call(s32[32,32]{1,0:T(8,128)} %ids_hbm.1, f32[32,32]{1,0:T(8,128)} %reader_hbm.1, bf16[2048,768]{1,0:T(8,128)(2,1)} %passages_ref.1), custom_call_target="tpu_custom_call" | custom-call | tf_op jit(solution)/shard_map/prepare/pallas_call | solution.py:207
  16.0 7.8 %all-to-all-done = s32[128,1,128]{2,1,0:T(1,128)S(1)} async-done(((s32[128,1,128]{2,1,0:T(1,128)}), s32[128,1,128]{2,1,0:T(1,128)S(1)}, u32[]{:S(2)}, u32[]{:S(2)}) %all-to-all-start) | async-done | bytes 65568 | tf_op jit(solution)/shard_map/all_to_all | solution.py:29
  23.8 2.8 %fetch.1 = bf16[2048,768]{1,0:T(8,128)(2,1)S(1)} custom-call(s32[128,128]{1,0:T(8,128)S(1)} %bitcast.14, bf16[2048,768]{1,0:T(8,128)(2,1)S(1)} %get-tuple-element.6.passages_ref), custom_call_target="tpu_custom_call" | custom-call | tf_op jit(solution)/shard_map/fetch/pallas_call | solution.py:223
  26.6 0.0 copy-start.1
  26.6 44.6 %all_to_all.25 = bf16[128,16,768]{2,1,0:T(8,128)(2,1)S(1)} all-to-all(bf16[128,16,768]{2,1,0:T(8,128)(2,1)S(1)} %bitcast.13), channel_id=1, replica_groups=mesh['index'=8,'bulk'=16] {'index','bulk'}, dimensions={0} | all-to-all | bytes 6291456 | tf_op jit(solution)/shard_map/all_to_all | solution.py:29
  71.2 0.0 copy-done.1
  71.2 1.9 %score.1 = (f32[32,2048]{1,0:T(8,128)S(1)}, f32[128,128]{1,0:T(8,128)}) custom-call(bf16[32,768]{1,0:T(8,128)(2,1)S(1)} %copy-done.1, bf16[2048,768]{1,0:T(8,128)(2,1)S(1)} %bitcast.11, f32[8,2048]{1,0:T(8,128)S(1)} %get-tuple-element.7.info_ref), custom_call_target="tpu_custom_call" | custom-call | tf_op jit(solution)/shard_map/score/pallas_call | solution.py:241
  73.1 4.9 %all-to-all-start.2 = ((f32[128,1,128]{2,1,0:T(1,128)}), f32[128,1,128]{2,1,0:T(1,128)S(1)}, u32[]{:S(2)}, u32[]{:S(2)}) async-start(f32[128,1,128]{2,1,0:T(1,128)} %bitcast.6), calls=%async_computation.2 | async-start | bytes 131072 | tf_op jit(solution)/shard_map/all_to_all | solution.py:29
  78.0 1.3 %grads.1 = f32[32,768]{1,0:T(8,128)} custom-call(f32[32,2048]{1,0:T(8,128)S(1)} %get-tuple-element.9.logs_ref, f32[8,2048]{1,0:T(8,128)S(1)} %get-tuple-element.7.info_ref, bf16[2048,768]{1,0:T(8,128)(2,1)S(1)} %bitcast.12), custom_call_target="tpu_custom_call" | custom-call | tf_op jit(solution)/shard_map/grads/pallas_call | solution.py:253
  79.2 8.5 %all-to-all-done.2 = f32[128,1,128]{2,1,0:T(1,128)S(1)} async-done(((f32[128,1,128]{2,1,0:T(1,128)}), f32[128,1,128]{2,1,0:T(1,128)S(1)}, u32[]{:S(2)}, u32[]{:S(2)}) %all-to-all-start.2) | async-done | bytes 65568 | tf_op jit(solution)/shard_map/all_to_all | solution.py:29
  87.8 0.7 reduce_sum.9
Async XLA Ops:
  0.6 0.7 copy-start
  2.5 21.2 %all-to-all-start = ((s32[128,1,128]{2,1,0:T(1,128)}), s32[128,1,128]{2,1,0:T(1,128)S(1)}, u32[]{:S(2)}, u32[]{:S(2)}) async-start(s32[128,1,128]{2,1,0:T(1,128)} %bitcast.1), calls=%async_computation | async-start | bytes 131072 | tf_op jit(solution)/shard_map/all_to_all | solution.py:29
  26.6 44.6 %copy-start.1 = (bf16[32,768]{1,0:T(8,128)(2,1)S(1)}, bf16[32,768]{1,0:T(8,128)(2,1)}, u32[]{:S(2)}) copy-start(bf16[32,768]{1,0:T(8,128)(2,1)} %questions_ref.1) | copy-start | bytes 147460
  73.1 14.7 %all-to-all-start.2 = ((f32[128,1,128]{2,1,0:T(1,128)}), f32[128,1,128]{2,1,0:T(1,128)S(1)}, u32[]{:S(2)}, u32[]{:S(2)}) async-start(f32[128,1,128]{2,1,0:T(1,128)} %bitcast.6), calls=%async_computation.2 | async-start | bytes 131072 | tf_op jit(solution)/shard_map/all_to_all | solution.py:29

commit v7 on v6

--- a/solution.py
+++ b/solution.py
@@ -78,16 +78,8 @@
     request_ref[...] = padded.T
 
 
-def prepare_kernel(
-    ids_hbm, reader_hbm, passages_ref, info_ref, local_ref, ids_ref, reader_scratch, sems
-):
-    pairs = ((reader_hbm, reader_scratch), (ids_hbm, ids_ref), (passages_ref, local_ref))
-    copies = [pltpu.make_async_copy(a, b, sems.at[n]) for n, (a, b) in enumerate(pairs)]
-    for copy in copies:
-        copy.start()
-    copies[0].wait()
-    reader_scratch[...] = log_normalize(reader_scratch[...])
-    copies[1].wait()
+def slot_maps(ids_ref, reader_ref, info_ref, reader_scratch):
+    reader_scratch[...] = log_normalize(reader_ref[...])
     ids = as_lanes(ids_ref)
     log_reader = as_lanes(reader_scratch)
     number = 4 * lax.broadcasted_iota(jnp.int32, (8, LANES), 0) + (
@@ -116,10 +108,23 @@
     reader = jnp.where(question >= 0.0, jnp.exp(log_reader), 0.0)
     rest = jnp.zeros((5, LANES * CAP), jnp.float32)
     info_ref[...] = jnp.concatenate([question, log_reader, reader, rest], axis=0)
-    copies[2].wait()
-
-
-def fetch_kernel(wanted_ref, passages_ref, rows_ref, image, even, odd, dense, index, sem):
+
+
+def fetch_kernel(
+    wanted_ref,
+    passages_ref,
+    ids_ref,
+    reader_ref,
+    rows_ref,
+    info_ref,
+    image,
+    even,
+    odd,
+    dense,
+    reader_scratch,
+    index,
+    sem,
+):
     count, width = passages_ref.shape
     chunks = width // LANES
     total = jnp.zeros((CAP, LANES), jnp.int32)
@@ -133,6 +138,7 @@
         image[c * STRIDE : c * STRIDE + count, :] = passages_ref[
             :, c * LANES : (c + 1) * LANES
         ].astype(jnp.float32)
+    slot_maps(ids_ref, reader_ref, info_ref, reader_scratch)
     copy.wait()
 
     def move(line, moved):
@@ -200,42 +206,31 @@
         out_shape=pltpu.VMEM((owners, LANES), jnp.int32),
         in_specs=[VMEM],
         out_specs=VMEM,
+        cost_estimate=pl.CostEstimate(flops=1 << 30, transcendentals=0, bytes_accessed=0),
         compiler_params=PARAMS,
         name="plan",
     )(candidate_ids)
     wanted = exchange(request)
-    info, local = pl.pallas_call(
-        prepare_kernel,
+    fetched, info = pl.pallas_call(
+        fetch_kernel,
         out_shape=(
+            pltpu.VMEM((slot_count, width), passages.dtype),
             pltpu.VMEM((8, slot_count), jnp.float32),
-            pltpu.VMEM(passages.shape, passages.dtype),
         ),
-        in_specs=[HBM, HBM, HBM],
+        in_specs=[VMEM, VMEM, VMEM, VMEM],
         out_specs=(VMEM, VMEM),
-        scratch_shapes=[
-            pltpu.VMEM(candidate_ids.shape, jnp.int32),
-            pltpu.VMEM(reader_loglik.shape, jnp.float32),
-            pltpu.SemaphoreType.DMA((3,)),
-        ],
-        compiler_params=PARAMS,
-        name="prepare",
-    )(in_hbm(candidate_ids), in_hbm(reader_loglik), in_hbm(passages))
-    fetched = pl.pallas_call(
-        fetch_kernel,
-        out_shape=pltpu.VMEM((slot_count, width), passages.dtype),
-        in_specs=[VMEM, VMEM],
-        out_specs=VMEM,
         scratch_shapes=[
             pltpu.VMEM((width // LANES * STRIDE, LANES), jnp.float32),
             pltpu.VMEM((width // LANES * STEP, LANES), jnp.float32),
             pltpu.VMEM((width // LANES * STEP, LANES), jnp.float32),
             pltpu.VMEM((CAP, LANES), jnp.int32),
+            pltpu.VMEM(reader_loglik.shape, jnp.float32),
             pltpu.SMEM((CAP, LANES), jnp.int32),
             pltpu.SemaphoreType.DMA,
         ],
         compiler_params=PARAMS,
         name="fetch",
-    )(wanted, in_vmem(local))
+    )(wanted, in_vmem(passages), in_vmem(candidate_ids), in_vmem(reader_loglik))
     replies = exchange(fetched.reshape(owners, CAP, width)).reshape(slot_count, width)
     replies = in_vmem(replies)
     logs, part = pl.pallas_call(

time: 88.7 us -> 88.6 us (level)
  blocking collectives: 44.6 us -> 65.7 us
  starting transfers between devices: 16.3 us -> 4.86 us
  waiting for transfers between devices: 16.3 us -> 8.54 us
  Pallas kernels: 9.1 us -> 7.11 us
    all_to_all x1 -> x2, blocking collectives: 44.6 us -> 65.7 us  [exchange(): return lax.all_to_all(blocks, AXES, split_axis=0, concat_axis=0, tiled=True)]
    all_to_all x2 -> x1, starting transfers between devices: 16.3 us -> 4.86 us  [exchange(): return lax.all_to_all(blocks, AXES, split_axis=0, concat_axis=0, tiled=True)]
    all_to_all x2 -> x1, waiting for transfers between devices: 16.3 us -> 8.54 us  [exchange(): return lax.all_to_all(blocks, AXES, split_axis=0, concat_axis=0, tiled=True)]
    pallas_call x2 -> x1, Pallas kernels: 4.77 us -> 3.41 us  [body(): pl.pallas_call(fetch_kernel, out_shape=(pltpu.VMEM((slot_count, width), p...]
  transfers between devices with their start and end apart: 2 -> 1, of which waited for: 2 -> 1; matrix products, arithmetic and copies ran while one was open for 0% -> 0% of each run, Pallas kernels for 4% -> 1%
where the time goes in v7:
time: 88.6 us; the launch traced here: 88.4 us
  blocking collectives  65.7 us (74%)
  waiting for transfers between devices  8.54 us (10%)
  Pallas kernels  7.11 us (8%)
  starting transfers between devices  4.86 us (5%)
    all_to_all x2, blocking collectives, exchange(): return lax.all_to_all(blocks, AXES, split_axis=0, concat_axis=0, tiled=True)  65.7 us
    all_to_all x1, waiting for transfers between devices, exchange(): return lax.all_to_all(blocks, AXES, split_axis=0, concat_axis=0, tiled=True)  8.54 us
    all_to_all x1, starting transfers between devices, exchange(): return lax.all_to_all(blocks, AXES, split_axis=0, concat_axis=0, tiled=True)  4.86 us
    pallas_call x1, Pallas kernels, body(): pl.pallas_call(fetch_kernel, out_shape=(pltpu.VMEM((slot_count, width), p...  3.41 us
    pallas_call x1, Pallas kernels, body(): pl.pallas_call(score_kernel, out_shape=(pltpu.VMEM((question_count, slot_...  1.89 us
  transfers between devices with their start and end apart: 1, of which 1 were waited for; matrix products, arithmetic and copies ran while one was open for 0% of the time, Pallas kernels for 1%

profile of v7, /device:TPU:1, one launch (start us, length us, event | category | flops | bytes accessed | tf_op | source)
XLA Modules:
  0.0 88.4 jit_solution(5698937691949271060)
XLA Ops:
  0.6 0.0 copy-start
  0.6 0.0 copy-start.2
  0.7 0.9 copy-done.2
  1.5 0.0 copy-start.3
  1.5 0.6 plan.1
  2.1 21.1 %all_to_all.25 = s32[128,1,128]{2,1,0:T(1,128)S(1)} all-to-all(s32[128,1,128]{2,1,0:T(1,128)S(1)} %bitcast.15), channel_id=1, replica_groups=mesh['index'=8,'bulk'=16] {'index','bulk'}, dimensions={0} | all-to-all | bytes 131072 | tf_op jit(solution)/shard_map/all_to_all | solution.py:29
  23.2 0.0 copy-done
  23.2 0.0 copy-done.3
  23.2 3.4 %fetch.1 = (bf16[2048,768]{1,0:T(8,128)(2,1)S(1)}, f32[8,2048]{1,0:T(8,128)S(1)}) custom-call(s32[128,128]{1,0:T(8,128)S(1)} %bitcast.14, bf16[2048,768]{1,0:T(8,128)(2,1)S(1)} %copy-done, s32[32,32]{1,0:T(8,128)S(1)} %copy-done.2, f32[32,32]{1,0:T(8,128)S(1)} %copy-done.3), custom_call_target="tpu_custom_call" | custom-call | tf_op jit(solution)/shard_map/fetch/pallas_call | solution.py:214
  26.6 0.0 copy-start.1
  26.6 44.6 %all_to_all.26 = bf16[128,16,768]{2,1,0:T(8,128)(2,1)S(1)} all-to-all(bf16[128,16,768]{2,1,0:T(8,128)(2,1)S(1)} %bitcast.13), channel_id=1, replica_groups=mesh['index'=8,'bulk'=16] {'index','bulk'}, dimensions={0} | all-to-all | bytes 6291456 | tf_op jit(solution)/shard_map/all_to_all | solution.py:29
  71.2 0.0 copy-done.1
  71.2 1.9 %score.1 = (f32[32,2048]{1,0:T(8,128)S(1)}, f32[128,128]{1,0:T(8,128)}) custom-call(bf16[32,768]{1,0:T(8,128)(2,1)S(1)} %copy-done.1, bf16[2048,768]{1,0:T(8,128)(2,1)S(1)} %bitcast.11, f32[8,2048]{1,0:T(8,128)S(1)} %get-tuple-element.7.info_ref), custom_call_target="tpu_custom_call" | custom-call | tf_op jit(solution)/shard_map/score/pallas_call | solution.py:236
  73.1 4.9 %all-to-all-start.2 = ((f32[128,1,128]{2,1,0:T(1,128)}), f32[128,1,128]{2,1,0:T(1,128)S(1)}, u32[]{:S(2)}, u32[]{:S(2)}) async-start(f32[128,1,128]{2,1,0:T(1,128)} %bitcast.6), calls=%async_computation.2 | async-start | bytes 131072 | tf_op jit(solution)/shard_map/all_to_all | solution.py:29
  78.0 1.3 %grads.1 = f32[32,768]{1,0:T(8,128)} custom-call(f32[32,2048]{1,0:T(8,128)S(1)} %get-tuple-element.9.logs_ref, f32[8,2048]{1,0:T(8,128)S(1)} %get-tuple-element.7.info_ref, bf16[2048,768]{1,0:T(8,128)(2,1)S(1)} %bitcast.12), custom_call_target="tpu_custom_call" | custom-call | tf_op jit(solution)/shard_map/grads/pallas_call | solution.py:248
  79.2 8.5 %all-to-all-done.2 = f32[128,1,128]{2,1,0:T(1,128)S(1)} async-done(((f32[128,1,128]{2,1,0:T(1,128)}), f32[128,1,128]{2,1,0:T(1,128)S(1)}, u32[]{:S(2)}, u32[]{:S(2)}) %all-to-all-start.2) | async-done | bytes 65568 | tf_op jit(solution)/shard_map/all_to_all | solution.py:29
  87.8 0.7 reduce_sum.9
Async XLA Ops:
  0.6 22.5 %copy-start = (bf16[2048,768]{1,0:T(8,128)(2,1)S(1)}, bf16[2048,768]{1,0:T(8,128)(2,1)}, u32[]{:S(2)}) copy-start(bf16[2048,768]{1,0:T(8,128)(2,1)} %passages_ref.1) | copy-start | bytes 9437188
  0.6 0.9 copy-start.2
  1.5 21.7 %copy-start.3 = (f32[32,32]{1,0:T(8,128)S(1)}, f32[32,32]{1,0:T(8,128)}, u32[]{:S(2)}) copy-start(f32[32,32]{1,0:T(8,128)} %reader_ref.1) | copy-start | bytes 12292
  26.6 44.6 %copy-start.1 = (bf16[32,768]{1,0:T(8,128)(2,1)S(1)}, bf16[32,768]{1,0:T(8,128)(2,1)}, u32[]{:S(2)}) copy-start(bf16[32,768]{1,0:T(8,128)(2,1)} %questions_ref.1) | copy-start | bytes 147460
  73.1 14.7 %all-to-all-start.2 = ((f32[128,1,128]{2,1,0:T(1,128)}), f32[128,1,128]{2,1,0:T(1,128)S(1)}, u32[]{:S(2)}, u32[]{:S(2)}) async-start(f32[128,1,128]{2,1,0:T(1,128)} %bitcast.6), calls=%async_computation.2 | async-start | bytes 131072 | tf_op jit(solution)/shard_map/all_to_all | solution.py:29

commit v8 on v7

--- a/solution.py
+++ b/solution.py
@@ -44,7 +44,7 @@
     return [jnp.where(owner[a : a + 1, :] == owners, 1.0, 0.0) for a in range(8)]
 
 
-def placements(member, values):
+def placement_stages(member, values):
     before = lax.broadcasted_iota(jnp.int32, (LANES, LANES), 0)
     after = lax.broadcasted_iota(jnp.int32, (LANES, LANES), 1)
     prefix = jnp.where(before < after, 1.0, 0.0).astype(jnp.bfloat16)
@@ -52,6 +52,7 @@
     for m in member:
         above.append(above[-1] + m)
     left_of = jnp.dot(above[8].astype(jnp.bfloat16), prefix, preferred_element_type=jnp.float32)
+    yield
     places = lax.broadcasted_iota(jnp.int32, (CAP, LANES), 0).astype(jnp.float32)
     left = []
     for a in range(8):
@@ -59,6 +60,7 @@
         here = jnp.where(places == place, 1.0, 0.0)
         pieces = [here * v[a : a + 1, :] for v in values]
         left.append(jnp.concatenate(pieces, axis=0).astype(jnp.bfloat16))
+    yield
     return lax.dot_general(
         jnp.concatenate(left, axis=1),
         jnp.concatenate([m.astype(jnp.bfloat16) for m in member], axis=1),
@@ -67,8 +69,18 @@
     )
 
 
-def plan_kernel(ids_ref, request_ref):
+def placements(member, values):
+    stages = placement_stages(member, values)
+    while True:
+        try:
+            next(stages)
+        except StopIteration as stop:
+            return stop.value
+
+
+def plan_kernel(ids_ref, request_ref, lanes_ref):
     ids = as_lanes(ids_ref)
+    lanes_ref[...] = ids
     row = ids & 2047
     high = (row >> 4).astype(jnp.float32)
     low = (row & 15).astype(jnp.float32)
@@ -78,9 +90,9 @@
     request_ref[...] = padded.T
 
 
-def slot_maps(ids_ref, reader_ref, info_ref, reader_scratch):
+def slot_stages(ids_ref, reader_ref, info_ref, reader_scratch):
     reader_scratch[...] = log_normalize(reader_ref[...])
-    ids = as_lanes(ids_ref)
+    yield
     log_reader = as_lanes(reader_scratch)
     number = 4 * lax.broadcasted_iota(jnp.int32, (8, LANES), 0) + (
         lax.broadcasted_iota(jnp.int32, (8, LANES), 1) >> 5
@@ -89,25 +101,34 @@
     rest = log_reader - part0
     part1 = rest.astype(jnp.bfloat16).astype(jnp.float32)
     part2 = rest - part1
-    table = placements(
-        members(ids >> 11), [(number + 1).astype(jnp.float32), part0, part1, part2]
-    )
-    owners = lax.broadcasted_iota(jnp.int32, (LANES, LANES * CAP), 0)
-    lanes = lax.broadcasted_iota(jnp.int32, (LANES, LANES * CAP), 1)
-    spread = jnp.where((lanes >> 4) == owners, 1.0, 0.0).astype(jnp.bfloat16)
-    wide = jnp.dot(table.astype(jnp.bfloat16), spread, preferred_element_type=jnp.float32)
-    own = (lanes[:CAP] & (CAP - 1)) == owners[:CAP]
-
-    def pick(n):
-        return jnp.sum(
-            jnp.where(own, wide[n * CAP : (n + 1) * CAP, :], 0.0), axis=0, keepdims=True
+    yield
+    member = members(ids_ref[...] >> 11)
+    yield
+    values = [(number + 1).astype(jnp.float32), part0, part1, part2]
+    table = yield from placement_stages(member, values)
+    table = table.astype(jnp.bfloat16)
+    yield
+    wide_count = LANES * CAP // 4
+    for n in range(4):
+        start = n * wide_count
+        owners = lax.broadcasted_iota(jnp.int32, (LANES, wide_count), 0)
+        lanes = lax.broadcasted_iota(jnp.int32, (LANES, wide_count), 1) + start
+        spread = jnp.where((lanes >> 4) == owners, 1.0, 0.0).astype(jnp.bfloat16)
+        wide = jnp.dot(table, spread, preferred_element_type=jnp.float32)
+        yield
+        own = (lanes[:CAP] & (CAP - 1)) == owners[:CAP]
+        picked = [
+            jnp.sum(jnp.where(own, wide[m * CAP : (m + 1) * CAP, :], 0.0), axis=0, keepdims=True)
+            for m in range(4)
+        ]
+        question = picked[0] - 1.0
+        log_part = picked[1] + picked[2] + picked[3]
+        reader = jnp.where(question >= 0.0, jnp.exp(log_part), 0.0)
+        fill = jnp.zeros((5, wide_count), jnp.float32)
+        info_ref[:, start : start + wide_count] = jnp.concatenate(
+            [question, log_part, reader, fill], axis=0
         )
-
-    question = pick(0) - 1.0
-    log_reader = pick(1) + pick(2) + pick(3)
-    reader = jnp.where(question >= 0.0, jnp.exp(log_reader), 0.0)
-    rest = jnp.zeros((5, LANES * CAP), jnp.float32)
-    info_ref[...] = jnp.concatenate([question, log_reader, reader, rest], axis=0)
+        yield
 
 
 def fetch_kernel(
@@ -138,7 +159,8 @@
         image[c * STRIDE : c * STRIDE + count, :] = passages_ref[
             :, c * LANES : (c + 1) * LANES
         ].astype(jnp.float32)
-    slot_maps(ids_ref, reader_ref, info_ref, reader_scratch)
+    stages = slot_stages(ids_ref, reader_ref, info_ref, reader_scratch)
+    next(stages)
     copy.wait()
 
     def move(line, moved):
@@ -156,7 +178,10 @@
     move(0, even)
     for line in range(1, CAP):
         move(line, buffers[line % 2])
+        next(stages, None)
         pack(line - 1, buffers[(line - 1) % 2])
+    for _ in stages:
+        pass
     pack(CAP - 1, odd)
 
 
@@ -201,11 +226,11 @@
     owners = lax.axis_size(AXES)
     question_count, width = questions.shape
     slot_count = owners * CAP
-    request = pl.pallas_call(
+    request, lanes = pl.pallas_call(
         plan_kernel,
-        out_shape=pltpu.VMEM((owners, LANES), jnp.int32),
+        out_shape=(pltpu.VMEM((owners, LANES), jnp.int32), pltpu.VMEM((8, LANES), jnp.int32)),
         in_specs=[VMEM],
-        out_specs=VMEM,
+        out_specs=(VMEM, VMEM),
         cost_estimate=pl.CostEstimate(flops=1 << 30, transcendentals=0, bytes_accessed=0),
         compiler_params=PARAMS,
         name="plan",
@@ -230,7 +255,7 @@
         ],
         compiler_params=PARAMS,
         name="fetch",
-    )(wanted, in_vmem(passages), in_vmem(candidate_ids), in_vmem(reader_loglik))
+    )(wanted, in_vmem(passages), in_vmem(lanes), in_vmem(reader_loglik))
     replies = exchange(fetched.reshape(owners, CAP, width)).reshape(slot_count, width)
     replies = in_vmem(replies)
     logs, part = pl.pallas_call(

time: 88.6 us -> 88.4 us (level)
  no operation moved by 1% of the time
where the time goes in v8:
time: 88.4 us; the launch traced here: 88.2 us
  blocking collectives  65.7 us (74%)
  waiting for transfers between devices  8.56 us (10%)
  Pallas kernels  6.84 us (8%)
  starting transfers between devices  4.86 us (5%)
    all_to_all x2, blocking collectives, exchange(): return lax.all_to_all(blocks, AXES, split_axis=0, concat_axis=0, tiled=True)  65.7 us
    all_to_all x1, waiting for transfers between devices, exchange(): return lax.all_to_all(blocks, AXES, split_axis=0, concat_axis=0, tiled=True)  8.56 us
    all_to_all x1, starting transfers between devices, exchange(): return lax.all_to_all(blocks, AXES, split_axis=0, concat_axis=0, tiled=True)  4.86 us
    pallas_call x1, Pallas kernels, body(): pl.pallas_call(fetch_kernel, out_shape=(pltpu.VMEM((slot_count, width), p...  3.13 us
    pallas_call x1, Pallas kernels, body(): pl.pallas_call(score_kernel, out_shape=(pltpu.VMEM((question_count, slot_...  1.91 us
  transfers between devices with their start and end apart: 1, of which 1 were waited for; matrix products, arithmetic and copies ran while one was open for 0% of the time, Pallas kernels for 1%

profile of v8, /device:TPU:1, one launch (start us, length us, event | category | flops | bytes accessed | tf_op | source)
XLA Modules:
  0.0 88.2 jit_solution(12747538268621382620)
XLA Ops:
  0.6 0.0 copy-start.2
  0.6 0.0 copy-start
  0.7 0.0 copy-start.3
  0.7 0.9 copy-done.3
  1.5 0.6 plan.1
  2.1 21.1 %all_to_all.25 = s32[128,1,128]{2,1,0:T(1,128)S(1)} all-to-all(s32[128,1,128]{2,1,0:T(1,128)S(1)} %bitcast.15), channel_id=1, replica_groups=mesh['index'=8,'bulk'=16] {'index','bulk'}, dimensions={0} | all-to-all | bytes 131072 | tf_op jit(solution)/shard_map/all_to_all | solution.py:29
  23.2 0.0 copy-done.2
  23.2 0.0 copy-done
  23.2 3.1 %fetch.1 = (bf16[2048,768]{1,0:T(8,128)(2,1)S(1)}, f32[8,2048]{1,0:T(8,128)S(1)}) custom-call(s32[128,128]{1,0:T(8,128)S(1)} %bitcast.14, bf16[2048,768]{1,0:T(8,128)(2,1)S(1)} %copy-done, s32[8,128]{1,0:T(8,128)S(1)} %get-tuple-element.9.ids_ref, f32[32,32]{1,0:T(8,128)S(1)} %copy-done.2), custom_call_target="tpu_custom_call" | custom-call | tf_op jit(solution)/shard_map/fetch/pallas_call | solution.py:239
  26.3 0.0 copy-start.1
  26.3 44.6 %all_to_all.26 = bf16[128,16,768]{2,1,0:T(8,128)(2,1)S(1)} all-to-all(bf16[128,16,768]{2,1,0:T(8,128)(2,1)S(1)} %bitcast.13), channel_id=1, replica_groups=mesh['index'=8,'bulk'=16] {'index','bulk'}, dimensions={0} | all-to-all | bytes 6291456 | tf_op jit(solution)/shard_map/all_to_all | solution.py:29
  70.9 0.0 copy-done.1
  70.9 1.9 %score.1 = (f32[32,2048]{1,0:T(8,128)S(1)}, f32[128,128]{1,0:T(8,128)}) custom-call(bf16[32,768]{1,0:T(8,128)(2,1)S(1)} %copy-done.1, bf16[2048,768]{1,0:T(8,128)(2,1)S(1)} %bitcast.11, f32[8,2048]{1,0:T(8,128)S(1)} %get-tuple-element.11.info_ref), custom_call_target="tpu_custom_call" | custom-call | tf_op jit(solution)/shard_map/score/pallas_call | solution.py:261
  72.8 4.9 %all-to-all-start.2 = ((f32[128,1,128]{2,1,0:T(1,128)}), f32[128,1,128]{2,1,0:T(1,128)S(1)}, u32[]{:S(2)}, u32[]{:S(2)}) async-start(f32[128,1,128]{2,1,0:T(1,128)} %bitcast.6), calls=%async_computation.2 | async-start | bytes 131072 | tf_op jit(solution)/shard_map/all_to_all | solution.py:29
  77.7 1.3 %grads.1 = f32[32,768]{1,0:T(8,128)} custom-call(f32[32,2048]{1,0:T(8,128)S(1)} %get-tuple-element.13.logs_ref, f32[8,2048]{1,0:T(8,128)S(1)} %get-tuple-element.11.info_ref, bf16[2048,768]{1,0:T(8,128)(2,1)S(1)} %bitcast.12), custom_call_target="tpu_custom_call" | custom-call | tf_op jit(solution)/shard_map/grads/pallas_call | solution.py:273
  79.0 8.6 %all-to-all-done.2 = f32[128,1,128]{2,1,0:T(1,128)S(1)} async-done(((f32[128,1,128]{2,1,0:T(1,128)}), f32[128,1,128]{2,1,0:T(1,128)S(1)}, u32[]{:S(2)}, u32[]{:S(2)}) %all-to-all-start.2) | async-done | bytes 65568 | tf_op jit(solution)/shard_map/all_to_all | solution.py:29
  87.5 0.7 reduce_sum.9
Async XLA Ops:
  0.6 22.5 %copy-start.2 = (f32[32,32]{1,0:T(8,128)S(1)}, f32[32,32]{1,0:T(8,128)}, u32[]{:S(2)}) copy-start(f32[32,32]{1,0:T(8,128)} %reader_ref.1) | copy-start | bytes 12292
  0.6 22.5 %copy-start = (bf16[2048,768]{1,0:T(8,128)(2,1)S(1)}, bf16[2048,768]{1,0:T(8,128)(2,1)}, u32[]{:S(2)}) copy-start(bf16[2048,768]{1,0:T(8,128)(2,1)} %passages_ref.1) | copy-start | bytes 9437188
  0.7 0.9 copy-start.3
  26.3 44.6 %copy-start.1 = (bf16[32,768]{1,0:T(8,128)(2,1)S(1)}, bf16[32,768]{1,0:T(8,128)(2,1)}, u32[]{:S(2)}) copy-start(bf16[32,768]{1,0:T(8,128)(2,1)} %questions_ref.1) | copy-start | bytes 147460
  72.8 14.7 %all-to-all-start.2 = ((f32[128,1,128]{2,1,0:T(1,128)}), f32[128,1,128]{2,1,0:T(1,128)S(1)}, u32[]{:S(2)}, u32[]{:S(2)}) async-start(f32[128,1,128]{2,1,0:T(1,128)} %bitcast.6), calls=%async_computation.2 | async-start | bytes 131072 | tf_op jit(solution)/shard_map/all_to_all | solution.py:29

commit v9 on v8

--- a/solution.py
+++ b/solution.py
@@ -185,7 +185,7 @@
     pack(CAP - 1, odd)
 
 
-def score_kernel(questions_ref, rows_ref, info_ref, logs_ref, part_ref):
+def score_kernel(questions_ref, rows_ref, info_ref, grads_ref, part_ref):
     count, width = questions_ref.shape
     scale = 4.0 / math.sqrt(width)
     scores = (
@@ -206,20 +206,16 @@
     known = jnp.sum(reader * (log_reader - own), axis=1, keepdims=True)
     mass = jnp.sum(jnp.where(mine, reader, 0.0), axis=1, keepdims=True)
     log_total = jnp.log(jnp.sum(jnp.exp(shifted), axis=1, keepdims=True))
-    logs_ref[...] = shifted - log_total
+    weights = jnp.where(mine, jnp.exp(shifted - log_total) - reader, 0.0).astype(jnp.bfloat16)
+    grads_ref[...] = jnp.dot(weights, rows_ref[...], preferred_element_type=jnp.float32) * scale
     divergence = known + jnp.sum(mass * log_total, axis=0, keepdims=True)
     total = divergence / (count * part_ref.shape[0])
     part_ref[...] = jnp.broadcast_to(total, part_ref.shape)
 
 
-def grads_kernel(logs_ref, info_ref, rows_ref, grads_ref):
-    scale = 4.0 / math.sqrt(rows_ref.shape[1])
-    mine = info_ref[0:1, :] == lax.broadcasted_iota(jnp.int32, logs_ref.shape, 0).astype(
-        jnp.float32
-    )
-    gap = jnp.exp(logs_ref[...]) - info_ref[2:3, :]
-    weights = jnp.where(mine, gap, 0.0).astype(jnp.bfloat16)
-    grads_ref[...] = jnp.dot(weights, rows_ref[...], preferred_element_type=jnp.float32) * scale
+def finish_kernel(sums_ref, local_ref, mean_ref, grads_ref):
+    grads_ref[...] = local_ref[...]
+    mean_ref[...] = jnp.sum(sums_ref[...], axis=0, keepdims=True)[:, :1]
 
 
 def body(questions, passages, candidate_ids, reader_loglik):
@@ -258,10 +254,10 @@
     )(wanted, in_vmem(passages), in_vmem(lanes), in_vmem(reader_loglik))
     replies = exchange(fetched.reshape(owners, CAP, width)).reshape(slot_count, width)
     replies = in_vmem(replies)
-    logs, part = pl.pallas_call(
+    grads, part = pl.pallas_call(
         score_kernel,
         out_shape=(
-            pltpu.VMEM((question_count, slot_count), jnp.float32),
+            pltpu.VMEM((question_count, width), jnp.float32),
             pltpu.VMEM((owners, LANES), jnp.float32),
         ),
         in_specs=[VMEM, VMEM, VMEM],
@@ -269,16 +265,18 @@
         compiler_params=PARAMS,
         name="score",
     )(questions, replies, info)
-    summed = exchange(part)
-    grads = pl.pallas_call(
-        grads_kernel,
-        out_shape=jax.ShapeDtypeStruct((question_count, width), jnp.float32),
-        in_specs=[VMEM, VMEM, VMEM],
-        out_specs=VMEM,
-        compiler_params=PARAMS,
-        name="grads",
-    )(logs, info, replies)
-    return (jnp.sum(summed, axis=0)[0], grads)
+    mean, out = pl.pallas_call(
+        finish_kernel,
+        out_shape=(
+            jax.ShapeDtypeStruct((1, 1), jnp.float32),
+            jax.ShapeDtypeStruct((question_count, width), jnp.float32),
+        ),
+        in_specs=[VMEM, VMEM],
+        out_specs=(VMEM, VMEM),
+        compiler_params=PARAMS,
+        name="finish",
+    )(exchange(part), in_vmem(grads))
+    return (mean.reshape(()), out)
 
 
 def solution(mesh):

time: 88.4 us -> 88.3 us (level)
  blocking collectives: 65.7 us -> 80.2 us
  waiting for transfers between devices: 8.56 us -> 0 us
  starting transfers between devices: 4.86 us -> 0 us
    all_to_all x2 -> x3, blocking collectives: 65.7 us -> 80.2 us  [exchange(): return lax.all_to_all(blocks, AXES, split_axis=0, concat_axis=0, tiled=True)]
    all_to_all x1 -> x0, waiting for transfers between devices: 8.56 us -> none  [exchange(): return lax.all_to_all(blocks, AXES, split_axis=0, concat_axis=0, tiled=True)]
    all_to_all x1 -> x0, starting transfers between devices: 4.86 us -> none  [exchange(): return lax.all_to_all(blocks, AXES, split_axis=0, concat_axis=0, tiled=True)]
  transfers between devices with their start and end apart: 1 -> 0, of which waited for: 1 -> 0; matrix products, arithmetic and copies ran while one was open for 0% -> 0% of each run, Pallas kernels for 1% -> 0%
where the time goes in v9:
time: 88.3 us; the launch traced here: 88.1 us
  blocking collectives  80.2 us (91%)
  Pallas kernels  6.35 us (7%)
    all_to_all x3, blocking collectives, exchange(): return lax.all_to_all(blocks, AXES, split_axis=0, concat_axis=0, tiled=True)  80.2 us
    pallas_call x1, Pallas kernels, body(): pl.pallas_call(fetch_kernel, out_shape=(pltpu.VMEM((slot_count, width), p...  3.1 us
    pallas_call x1, Pallas kernels, body(): pl.pallas_call(score_kernel, out_shape=(pltpu.VMEM((question_count, width...  2.05 us

profile of v9, /device:TPU:1, one launch (start us, length us, event | category | flops | bytes accessed | tf_op | source)
XLA Modules:
  0.0 88.1 jit_solution(5874308925503006680)
XLA Ops:
  0.6 0.0 copy-start.2
  0.6 0.0 copy-start
  0.7 0.0 copy-start.3
  0.7 0.9 copy-done.3
  1.5 0.6 plan.1
  2.1 21.1 %all_to_all.27 = s32[128,1,128]{2,1,0:T(1,128)S(1)} all-to-all(s32[128,1,128]{2,1,0:T(1,128)S(1)} %bitcast.16), channel_id=1, replica_groups=mesh['index'=8,'bulk'=16] {'index','bulk'}, dimensions={0} | all-to-all | bytes 131072 | tf_op jit(solution)/shard_map/all_to_all | solution.py:29
  23.2 0.0 copy-done.2
  23.2 0.0 copy-done
  23.2 3.1 %fetch.1 = (bf16[2048,768]{1,0:T(8,128)(2,1)S(1)}, f32[8,2048]{1,0:T(8,128)S(1)}) custom-call(s32[128,128]{1,0:T(8,128)S(1)} %bitcast.13, bf16[2048,768]{1,0:T(8,128)(2,1)S(1)} %copy-done, s32[8,128]{1,0:T(8,128)S(1)} %get-tuple-element.11.ids_ref, f32[32,32]{1,0:T(8,128)S(1)} %copy-done.2), custom_call_target="tpu_custom_call" | custom-call | tf_op jit(solution)/shard_map/fetch/pallas_call | solution.py:235
  26.3 0.0 copy-start.1
  26.3 44.6 %all_to_all.28 = bf16[128,16,768]{2,1,0:T(8,128)(2,1)S(1)} all-to-all(bf16[128,16,768]{2,1,0:T(8,128)(2,1)S(1)} %bitcast.12), channel_id=1, replica_groups=mesh['index'=8,'bulk'=16] {'index','bulk'}, dimensions={0} | all-to-all | bytes 6291456 | tf_op jit(solution)/shard_map/all_to_all | solution.py:29
  70.9 0.0 copy-done.1
  70.9 2.0 %score.1 = (f32[32,768]{1,0:T(8,128)S(1)}, f32[128,128]{1,0:T(8,128)S(1)}) custom-call(bf16[32,768]{1,0:T(8,128)(2,1)S(1)} %copy-done.1, bf16[2048,768]{1,0:T(8,128)(2,1)S(1)} %bitcast.11, f32[8,2048]{1,0:T(8,128)S(1)} %get-tuple-element.13.info_ref), custom_call_target="tpu_custom_call" | custom-call | tf_op jit(solution)/shard_map/score/pallas_call | solution.py:257
  73.0 14.5 %all_to_all.29 = f32[128,1,128]{2,1,0:T(1,128)S(1)} all-to-all(f32[128,1,128]{2,1,0:T(1,128)S(1)} %bitcast.15), channel_id=1, replica_groups=mesh['index'=8,'bulk'=16] {'index','bulk'}, dimensions={0} | all-to-all | bytes 131072 | tf_op jit(solution)/shard_map/all_to_all | solution.py:29
  87.4 0.7 finish.1
Async XLA Ops:
  0.6 22.5 %copy-start.2 = (f32[32,32]{1,0:T(8,128)S(1)}, f32[32,32]{1,0:T(8,128)}, u32[]{:S(2)}) copy-start(f32[32,32]{1,0:T(8,128)} %reader_ref.1) | copy-start | bytes 12292
  0.6 22.5 %copy-start = (bf16[2048,768]{1,0:T(8,128)(2,1)S(1)}, bf16[2048,768]{1,0:T(8,128)(2,1)}, u32[]{:S(2)}) copy-start(bf16[2048,768]{1,0:T(8,128)(2,1)} %passages_ref.1) | copy-start | bytes 9437188
  0.7 0.9 copy-start.3
  26.3 44.6 %copy-start.1 = (bf16[32,768]{1,0:T(8,128)(2,1)S(1)}, bf16[32,768]{1,0:T(8,128)(2,1)}, u32[]{:S(2)}) copy-start(bf16[32,768]{1,0:T(8,128)(2,1)} %questions_ref.1) | copy-start | bytes 147460

commit v10 on v9

--- a/solution.py
+++ b/solution.py
@@ -185,18 +185,22 @@
     pack(CAP - 1, odd)
 
 
-def score_kernel(questions_ref, rows_ref, info_ref, grads_ref, part_ref):
+def inner(left, right):
+    return lax.dot_general(
+        left, right, (((1,), (1,)), ((), ())), preferred_element_type=jnp.float32
+    )
+
+
+def score_kernel(questions_ref, rows_ref, info_ref, weights_ref, part_ref):
     count, width = questions_ref.shape
     scale = 4.0 / math.sqrt(width)
-    scores = (
-        lax.dot_general(
-            questions_ref[...],
-            rows_ref[...],
-            (((1,), (1,)), ((), ())),
-            preferred_element_type=jnp.float32,
-        )
-        * scale
-    )
+    questions = questions_ref[...]
+    block = rows_ref.shape[0] // 8
+    pieces = []
+    for n in range(8):
+        rows = rows_ref[n * block : (n + 1) * block, :]
+        pieces.append(inner(rows, questions).T if n % 2 else inner(questions, rows))
+    scores = jnp.concatenate(pieces, axis=1) * scale
     log_reader = info_ref[1:2, :]
     reader = info_ref[2:3, :]
     mine = info_ref[0:1, :] == lax.broadcasted_iota(jnp.int32, scores.shape, 0).astype(jnp.float32)
@@ -206,16 +210,19 @@
     known = jnp.sum(reader * (log_reader - own), axis=1, keepdims=True)
     mass = jnp.sum(jnp.where(mine, reader, 0.0), axis=1, keepdims=True)
     log_total = jnp.log(jnp.sum(jnp.exp(shifted), axis=1, keepdims=True))
-    weights = jnp.where(mine, jnp.exp(shifted - log_total) - reader, 0.0).astype(jnp.bfloat16)
-    grads_ref[...] = jnp.dot(weights, rows_ref[...], preferred_element_type=jnp.float32) * scale
+    gap = jnp.exp(shifted - log_total) - reader
+    weights_ref[...] = jnp.where(mine, gap, 0.0).astype(jnp.bfloat16)
     divergence = known + jnp.sum(mass * log_total, axis=0, keepdims=True)
     total = divergence / (count * part_ref.shape[0])
     part_ref[...] = jnp.broadcast_to(total, part_ref.shape)
 
 
-def finish_kernel(sums_ref, local_ref, mean_ref, grads_ref):
-    grads_ref[...] = local_ref[...]
+def finish_kernel(sums_ref, weights_ref, rows_ref, mean_ref, grads_ref):
+    scale = 4.0 / math.sqrt(rows_ref.shape[1])
     mean_ref[...] = jnp.sum(sums_ref[...], axis=0, keepdims=True)[:, :1]
+    grads_ref[...] = (
+        jnp.dot(weights_ref[...], rows_ref[...], preferred_element_type=jnp.float32) * scale
+    )
 
 
 def body(questions, passages, candidate_ids, reader_loglik):
@@ -254,10 +261,10 @@
     )(wanted, in_vmem(passages), in_vmem(lanes), in_vmem(reader_loglik))
     replies = exchange(fetched.reshape(owners, CAP, width)).reshape(slot_count, width)
     replies = in_vmem(replies)
-    grads, part = pl.pallas_call(
+    weights, part = pl.pallas_call(
         score_kernel,
         out_shape=(
-            pltpu.VMEM((question_count, width), jnp.float32),
+            pltpu.VMEM((question_count, slot_count), jnp.bfloat16),
             pltpu.VMEM((owners, LANES), jnp.float32),
         ),
         in_specs=[VMEM, VMEM, VMEM],
@@ -265,18 +272,18 @@
         compiler_params=PARAMS,
         name="score",
     )(questions, replies, info)
-    mean, out = pl.pallas_call(
+    mean, grads = pl.pallas_call(
         finish_kernel,
         out_shape=(
             jax.ShapeDtypeStruct((1, 1), jnp.float32),
             jax.ShapeDtypeStruct((question_count, width), jnp.float32),
         ),
-        in_specs=[VMEM, VMEM],
+        in_specs=[VMEM, VMEM, VMEM],
         out_specs=(VMEM, VMEM),
         compiler_params=PARAMS,
         name="finish",
-    )(exchange(part), in_vmem(grads))
-    return (mean.reshape(()), out)
+    )(exchange(part), weights, replies)
+    return (mean.reshape(()), grads)
 
 
 def solution(mesh):

time: 88.3 us -> 88 us (level)
    pallas_call x1, Pallas kernels: 2.05 us -> 1.15 us  [body(): pl.pallas_call(score_kernel, out_shape=(pltpu.VMEM((question_count, slot_...]
where the time goes in v10:
time: 88 us; the launch traced here: 87.8 us
  blocking collectives  80.2 us (91%)
  Pallas kernels  6.08 us (7%)
  local copies, waits for them, and re-layouts  0.88 us (1%)
    all_to_all x3, blocking collectives, exchange(): return lax.all_to_all(blocks, AXES, split_axis=0, concat_axis=0, tiled=True)  80.2 us
    pallas_call x1, Pallas kernels, body(): pl.pallas_call(fetch_kernel, out_shape=(pltpu.VMEM((slot_count, width), p...  3.1 us

profile of v10, /device:TPU:1, one launch (start us, length us, event | category | flops | bytes accessed | tf_op | source)
XLA Modules:
  0.0 87.8 jit_solution(5318790530447036549)
XLA Ops:
  0.6 0.0 copy-start.2
  0.6 0.0 copy-start
  0.7 0.0 copy-start.3
  0.7 0.9 copy-done.3
  1.5 0.6 plan.1
  2.1 21.1 %all_to_all.27 = s32[128,1,128]{2,1,0:T(1,128)S(1)} all-to-all(s32[128,1,128]{2,1,0:T(1,128)S(1)} %bitcast.17), channel_id=1, replica_groups=mesh['index'=8,'bulk'=16] {'index','bulk'}, dimensions={0} | all-to-all | bytes 131072 | tf_op jit(solution)/shard_map/all_to_all | solution.py:29
  23.2 0.0 copy-done.2
  23.2 0.0 copy-done
  23.2 3.1 %fetch.1 = (bf16[2048,768]{1,0:T(8,128)(2,1)S(1)}, f32[8,2048]{1,0:T(8,128)S(1)}) custom-call(s32[128,128]{1,0:T(8,128)S(1)} %bitcast.15, bf16[2048,768]{1,0:T(8,128)(2,1)S(1)} %copy-done, s32[8,128]{1,0:T(8,128)S(1)} %get-tuple-element.11.ids_ref, f32[32,32]{1,0:T(8,128)S(1)} %copy-done.2), custom_call_target="tpu_custom_call" | custom-call | tf_op jit(solution)/shard_map/fetch/pallas_call | solution.py:242
  26.3 0.0 copy-start.1
  26.3 44.6 %all_to_all.28 = bf16[128,16,768]{2,1,0:T(8,128)(2,1)S(1)} all-to-all(bf16[128,16,768]{2,1,0:T(8,128)(2,1)S(1)} %bitcast.13), channel_id=1, replica_groups=mesh['index'=8,'bulk'=16] {'index','bulk'}, dimensions={0} | all-to-all | bytes 6291456 | tf_op jit(solution)/shard_map/all_to_all | solution.py:29
  70.9 0.0 copy-done.1
  70.9 1.1 %score.1 = (bf16[32,2048]{1,0:T(8,128)(2,1)S(1)}, f32[128,128]{1,0:T(8,128)S(1)}) custom-call(bf16[32,768]{1,0:T(8,128)(2,1)S(1)} %copy-done.1, bf16[2048,768]{1,0:T(8,128)(2,1)S(1)} %bitcast.11, f32[8,2048]{1,0:T(8,128)S(1)} %get-tuple-element.13.info_ref), custom_call_target="tpu_custom_call" | custom-call | tf_op jit(solution)/shard_map/score/pallas_call | solution.py:264
  72.1 14.5 %all_to_all.29 = f32[128,1,128]{2,1,0:T(1,128)S(1)} all-to-all(f32[128,1,128]{2,1,0:T(1,128)S(1)} %bitcast.16), channel_id=1, replica_groups=mesh['index'=8,'bulk'=16] {'index','bulk'}, dimensions={0} | all-to-all | bytes 131072 | tf_op jit(solution)/shard_map/all_to_all | solution.py:29
  86.5 1.3 %finish.1 = (f32[1,1]{1,0:T(1,128)}, f32[32,768]{1,0:T(8,128)}) custom-call(f32[128,128]{1,0:T(8,128)S(1)} %bitcast.14, bf16[32,2048]{1,0:T(8,128)(2,1)S(1)} %get-tuple-element.15.weights_ref, bf16[2048,768]{1,0:T(8,128)(2,1)S(1)} %bitcast.12), custom_call_target="tpu_custom_call" | custom-call | tf_op jit(solution)/shard_map/finish/pallas_call | solution.py:275
Async XLA Ops:
  0.6 22.5 %copy-start.2 = (f32[32,32]{1,0:T(8,128)S(1)}, f32[32,32]{1,0:T(8,128)}, u32[]{:S(2)}) copy-start(f32[32,32]{1,0:T(8,128)} %reader_ref.1) | copy-start | bytes 12292
  0.6 22.5 %copy-start = (bf16[2048,768]{1,0:T(8,128)(2,1)S(1)}, bf16[2048,768]{1,0:T(8,128)(2,1)}, u32[]{:S(2)}) copy-start(bf16[2048,768]{1,0:T(8,128)(2,1)} %passages_ref.1) | copy-start | bytes 9437188
  0.7 0.9 copy-start.3
  26.3 44.6 %copy-start.1 = (bf16[32,768]{1,0:T(8,128)(2,1)S(1)}, bf16[32,768]{1,0:T(8,128)(2,1)}, u32[]{:S(2)}) copy-start(bf16[32,768]{1,0:T(8,128)(2,1)} %questions_ref.1) | copy-start | bytes 147460

commit v11 on v10

--- a/solution.py
+++ b/solution.py
@@ -44,7 +44,7 @@
     return [jnp.where(owner[a : a + 1, :] == owners, 1.0, 0.0) for a in range(8)]
 
 
-def placement_stages(member, values):
+def place_onehots(member):
     before = lax.broadcasted_iota(jnp.int32, (LANES, LANES), 0)
     after = lax.broadcasted_iota(jnp.int32, (LANES, LANES), 1)
     prefix = jnp.where(before < after, 1.0, 0.0).astype(jnp.bfloat16)
@@ -52,15 +52,19 @@
     for m in member:
         above.append(above[-1] + m)
     left_of = jnp.dot(above[8].astype(jnp.bfloat16), prefix, preferred_element_type=jnp.float32)
-    yield
     places = lax.broadcasted_iota(jnp.int32, (CAP, LANES), 0).astype(jnp.float32)
+    onehots = []
+    for a in range(8):
+        place = jnp.sum(member[a] * (left_of + above[a]), axis=0, keepdims=True)
+        onehots.append(jnp.where(places == place, 1.0, 0.0))
+    return onehots
+
+
+def placed(member, onehots, values):
     left = []
     for a in range(8):
-        place = jnp.sum(member[a] * (left_of + above[a]), axis=0, keepdims=True)
-        here = jnp.where(places == place, 1.0, 0.0)
-        pieces = [here * v[a : a + 1, :] for v in values]
+        pieces = [onehots[a] * v[a : a + 1, :] for v in values]
         left.append(jnp.concatenate(pieces, axis=0).astype(jnp.bfloat16))
-    yield
     return lax.dot_general(
         jnp.concatenate(left, axis=1),
         jnp.concatenate([m.astype(jnp.bfloat16) for m in member], axis=1),
@@ -69,28 +73,23 @@
     )
 
 
-def placements(member, values):
-    stages = placement_stages(member, values)
-    while True:
-        try:
-            next(stages)
-        except StopIteration as stop:
-            return stop.value
-
-
-def plan_kernel(ids_ref, request_ref, lanes_ref):
+def plan_kernel(ids_ref, request_ref, lanes_ref, places_ref):
     ids = as_lanes(ids_ref)
     lanes_ref[...] = ids
     row = ids & 2047
     high = (row >> 4).astype(jnp.float32)
     low = (row & 15).astype(jnp.float32)
-    table = placements(members(ids >> 11), [high, low])
+    member = members(ids >> 11)
+    onehots = place_onehots(member)
+    for a in range(8):
+        places_ref[a * CAP : (a + 1) * CAP, :] = onehots[a]
+    table = placed(member, onehots, [high, low])
     wanted = (table[:CAP, :] * 16.0 + table[CAP:, :]).astype(jnp.int32)
     padded = jnp.concatenate([wanted, jnp.zeros((LANES - CAP, LANES), jnp.int32)], axis=0)
     request_ref[...] = padded.T
 
 
-def slot_stages(ids_ref, reader_ref, info_ref, reader_scratch):
+def slot_stages(ids_ref, places_ref, reader_ref, info_ref, reader_scratch):
     reader_scratch[...] = log_normalize(reader_ref[...])
     yield
     log_reader = as_lanes(reader_scratch)
@@ -105,8 +104,8 @@
     member = members(ids_ref[...] >> 11)
     yield
     values = [(number + 1).astype(jnp.float32), part0, part1, part2]
-    table = yield from placement_stages(member, values)
-    table = table.astype(jnp.bfloat16)
+    onehots = [places_ref[a * CAP : (a + 1) * CAP, :] for a in range(8)]
+    table = placed(member, onehots, values).astype(jnp.bfloat16)
     yield
     wide_count = LANES * CAP // 4
     for n in range(4):
@@ -135,6 +134,7 @@
     wanted_ref,
     passages_ref,
     ids_ref,
+    places_ref,
     reader_ref,
     rows_ref,
     info_ref,
@@ -159,7 +159,7 @@
         image[c * STRIDE : c * STRIDE + count, :] = passages_ref[
             :, c * LANES : (c + 1) * LANES
         ].astype(jnp.float32)
-    stages = slot_stages(ids_ref, reader_ref, info_ref, reader_scratch)
+    stages = slot_stages(ids_ref, places_ref, reader_ref, info_ref, reader_scratch)
     next(stages)
     copy.wait()
 
@@ -229,11 +229,15 @@
     owners = lax.axis_size(AXES)
     question_count, width = questions.shape
     slot_count = owners * CAP
-    request, lanes = pl.pallas_call(
+    request, lanes, places = pl.pallas_call(
         plan_kernel,
-        out_shape=(pltpu.VMEM((owners, LANES), jnp.int32), pltpu.VMEM((8, LANES), jnp.int32)),
+        out_shape=(
+            pltpu.VMEM((owners, LANES), jnp.int32),
+            pltpu.VMEM((8, LANES), jnp.int32),
+            pltpu.VMEM((8 * CAP, LANES), jnp.float32),
+        ),
         in_specs=[VMEM],
-        out_specs=(VMEM, VMEM),
+        out_specs=(VMEM, VMEM, VMEM),
         cost_estimate=pl.CostEstimate(flops=1 << 30, transcendentals=0, bytes_accessed=0),
         compiler_params=PARAMS,
         name="plan",
@@ -245,7 +249,7 @@
             pltpu.VMEM((slot_count, width), passages.dtype),
             pltpu.VMEM((8, slot_count), jnp.float32),
         ),
-        in_specs=[VMEM, VMEM, VMEM, VMEM],
+        in_specs=[VMEM, VMEM, VMEM, VMEM, VMEM],
         out_specs=(VMEM, VMEM),
         scratch_shapes=[
             pltpu.VMEM((width // LANES * STRIDE, LANES), jnp.float32),
@@ -258,7 +262,7 @@
         ],
         compiler_params=PARAMS,
         name="fetch",
-    )(wanted, in_vmem(passages), in_vmem(lanes), in_vmem(reader_loglik))
+    )(wanted, in_vmem(passages), in_vmem(lanes), in_vmem(places), in_vmem(reader_loglik))
     replies = exchange(fetched.reshape(owners, CAP, width)).reshape(slot_count, width)
     replies = in_vmem(replies)
     weights, part = pl.pallas_call(

time: 88 us -> 87.9 us (level)
  no operation moved by 1% of the time
where the time goes in v11:
time: 87.9 us; the launch traced here: 87.7 us
  blocking collectives  80.2 us (91%)
  Pallas kernels  5.96 us (7%)
  local copies, waits for them, and re-layouts  0.88 us (1%)
    all_to_all x3, blocking collectives, exchange(): return lax.all_to_all(blocks, AXES, split_axis=0, concat_axis=0, tiled=True)  80.2 us
    pallas_call x1, Pallas kernels, body(): pl.pallas_call(fetch_kernel, out_shape=(pltpu.VMEM((slot_count, width), p...  2.98 us

profile of v11, /device:TPU:1, one launch (start us, length us, event | category | flops | bytes accessed | tf_op | source)
XLA Modules:
  0.0 87.7 jit_solution(1478951258688901435)
XLA Ops:
  0.6 0.0 copy-start.2
  0.6 0.0 copy-start
  0.7 0.0 copy-start.3
  0.7 0.9 copy-done.3
  1.5 0.6 plan.1
  2.1 21.1 %all_to_all.27 = s32[128,1,128]{2,1,0:T(1,128)S(1)} all-to-all(s32[128,1,128]{2,1,0:T(1,128)S(1)} %bitcast.16), channel_id=1, replica_groups=mesh['index'=8,'bulk'=16] {'index','bulk'}, dimensions={0} | all-to-all | bytes 131072 | tf_op jit(solution)/shard_map/all_to_all | solution.py:29
  23.2 0.0 copy-done.2
  23.2 0.0 copy-done
  23.2 3.0 %fetch.1 = (bf16[2048,768]{1,0:T(8,128)(2,1)S(1)}, f32[8,2048]{1,0:T(8,128)S(1)}) custom-call(s32[128,128]{1,0:T(8,128)S(1)} %bitcast.14, bf16[2048,768]{1,0:T(8,128)(2,1)S(1)} %copy-done, s32[8,128]{1,0:T(8,128)S(1)} %get-tuple-element.12.ids_ref, f32[128,128]{1,0:T(8,128)S(1)} %get-tuple-element.13.places_ref, f32[32,32]{1,0:T(8,128)S(1)} %copy-done.2), custom_call_target="tpu_custom_call" | custom-call | tf_op jit(solution)/shard_map/fetch/pallas_call | solution.py:246
  26.2 0.0 copy-start.1
  26.2 44.6 %all_to_all.28 = bf16[128,16,768]{2,1,0:T(8,128)(2,1)S(1)} all-to-all(bf16[128,16,768]{2,1,0:T(8,128)(2,1)S(1)} %bitcast.13), channel_id=1, replica_groups=mesh['index'=8,'bulk'=16] {'index','bulk'}, dimensions={0} | all-to-all | bytes 6291456 | tf_op jit(solution)/shard_map/all_to_all | solution.py:29
  70.8 0.0 copy-done.1
  70.8 1.1 %score.1 = (bf16[32,2048]{1,0:T(8,128)(2,1)S(1)}, f32[128,128]{1,0:T(8,128)S(1)}) custom-call(bf16[32,768]{1,0:T(8,128)(2,1)S(1)} %copy-done.1, bf16[2048,768]{1,0:T(8,128)(2,1)S(1)} %bitcast.11, f32[8,2048]{1,0:T(8,128)S(1)} %get-tuple-element.15.info_ref), custom_call_target="tpu_custom_call" | custom-call | tf_op jit(solution)/shard_map/score/pallas_call | solution.py:268
  72.0 14.5 %all_to_all.29 = f32[128,1,128]{2,1,0:T(1,128)S(1)} all-to-all(f32[128,1,128]{2,1,0:T(1,128)S(1)} %bitcast.17), channel_id=1, replica_groups=mesh['index'=8,'bulk'=16] {'index','bulk'}, dimensions={0} | all-to-all | bytes 131072 | tf_op jit(solution)/shard_map/all_to_all | solution.py:29
  86.4 1.3 %finish.1 = (f32[1,1]{1,0:T(1,128)}, f32[32,768]{1,0:T(8,128)}) custom-call(f32[128,128]{1,0:T(8,128)S(1)} %bitcast.15, bf16[32,2048]{1,0:T(8,128)(2,1)S(1)} %get-tuple-element.17.weights_ref, bf16[2048,768]{1,0:T(8,128)(2,1)S(1)} %bitcast.12), custom_call_target="tpu_custom_call" | custom-call | tf_op jit(solution)/shard_map/finish/pallas_call | solution.py:279
Async XLA Ops:
  0.6 22.6 %copy-start.2 = (f32[32,32]{1,0:T(8,128)S(1)}, f32[32,32]{1,0:T(8,128)}, u32[]{:S(2)}) copy-start(f32[32,32]{1,0:T(8,128)} %reader_ref.1) | copy-start | bytes 12292
  0.6 22.5 %copy-start = (bf16[2048,768]{1,0:T(8,128)(2,1)S(1)}, bf16[2048,768]{1,0:T(8,128)(2,1)}, u32[]{:S(2)}) copy-start(bf16[2048,768]{1,0:T(8,128)(2,1)} %passages_ref.1) | copy-start | bytes 9437188
  0.7 0.9 copy-start.3
  26.2 44.6 %copy-start.1 = (bf16[32,768]{1,0:T(8,128)(2,1)S(1)}, bf16[32,768]{1,0:T(8,128)(2,1)}, u32[]{:S(2)}) copy-start(bf16[32,768]{1,0:T(8,128)(2,1)} %questions_ref.1) | copy-start | bytes 147460

commit v12 on v11

--- a/solution.py
+++ b/solution.py
@@ -105,17 +105,19 @@
     yield
     values = [(number + 1).astype(jnp.float32), part0, part1, part2]
     onehots = [places_ref[a * CAP : (a + 1) * CAP, :] for a in range(8)]
-    table = placed(member, onehots, values).astype(jnp.bfloat16)
+    table = placed(member, onehots, values)
     yield
-    wide_count = LANES * CAP // 4
+    group = LANES // 4
+    wide_count = group * CAP
+    owners = lax.broadcasted_iota(jnp.int32, (group, wide_count), 0)
+    lanes = lax.broadcasted_iota(jnp.int32, (group, wide_count), 1)
+    spread = jnp.where((lanes >> 4) == owners, 1.0, 0.0).astype(jnp.bfloat16)
+    own = (lanes[:CAP] & (CAP - 1)) == owners[:CAP]
     for n in range(4):
         start = n * wide_count
-        owners = lax.broadcasted_iota(jnp.int32, (LANES, wide_count), 0)
-        lanes = lax.broadcasted_iota(jnp.int32, (LANES, wide_count), 1) + start
-        spread = jnp.where((lanes >> 4) == owners, 1.0, 0.0).astype(jnp.bfloat16)
-        wide = jnp.dot(table, spread, preferred_element_type=jnp.float32)
+        part = table[:, n * group : (n + 1) * group].astype(jnp.bfloat16)
+        wide = jnp.dot(part, spread, preferred_element_type=jnp.float32)
         yield
-        own = (lanes[:CAP] & (CAP - 1)) == owners[:CAP]
         picked = [
             jnp.sum(jnp.where(own, wide[m * CAP : (m + 1) * CAP, :], 0.0), axis=0, keepdims=True)
             for m in range(4)

time: 87.9 us -> 87.9 us (level)
  no operation moved by 1% of the time
where the time goes in v12:
time: 87.9 us; the launch traced here: 87.7 us
  blocking collectives  80.2 us (91%)
  Pallas kernels  5.94 us (7%)
  local copies, waits for them, and re-layouts  0.88 us (1%)
    all_to_all x3, blocking collectives, exchange(): return lax.all_to_all(blocks, AXES, split_axis=0, concat_axis=0, tiled=True)  80.2 us
    pallas_call x1, Pallas kernels, body(): pl.pallas_call(fetch_kernel, out_shape=(pltpu.VMEM((slot_count, width), p...  2.95 us

profile of v12, /device:TPU:1, one launch (start us, length us, event | category | flops | bytes accessed | tf_op | source)
XLA Modules:
  0.0 87.7 jit_solution(3542454662549098372)
XLA Ops:
  0.6 0.0 copy-start.2
  0.6 0.0 copy-start
  0.7 0.0 copy-start.3
  0.7 0.9 copy-done.3
  1.5 0.6 plan.1
  2.1 21.1 %all_to_all.27 = s32[128,1,128]{2,1,0:T(1,128)S(1)} all-to-all(s32[128,1,128]{2,1,0:T(1,128)S(1)} %bitcast.16), channel_id=1, replica_groups=mesh['index'=8,'bulk'=16] {'index','bulk'}, dimensions={0} | all-to-all | bytes 131072 | tf_op jit(solution)/shard_map/all_to_all | solution.py:29
  23.2 0.0 copy-done.2
  23.2 0.0 copy-done
  23.2 3.0 %fetch.1 = (bf16[2048,768]{1,0:T(8,128)(2,1)S(1)}, f32[8,2048]{1,0:T(8,128)S(1)}) custom-call(s32[128,128]{1,0:T(8,128)S(1)} %bitcast.14, bf16[2048,768]{1,0:T(8,128)(2,1)S(1)} %copy-done, s32[8,128]{1,0:T(8,128)S(1)} %get-tuple-element.12.ids_ref, f32[128,128]{1,0:T(8,128)S(1)} %get-tuple-element.13.places_ref, f32[32,32]{1,0:T(8,128)S(1)} %copy-done.2), custom_call_target="tpu_custom_call" | custom-call | tf_op jit(solution)/shard_map/fetch/pallas_call | solution.py:248
  26.1 0.0 copy-start.1
  26.2 44.6 %all_to_all.28 = bf16[128,16,768]{2,1,0:T(8,128)(2,1)S(1)} all-to-all(bf16[128,16,768]{2,1,0:T(8,128)(2,1)S(1)} %bitcast.13), channel_id=1, replica_groups=mesh['index'=8,'bulk'=16] {'index','bulk'}, dimensions={0} | all-to-all | bytes 6291456 | tf_op jit(solution)/shard_map/all_to_all | solution.py:29
  70.8 0.0 copy-done.1
  70.8 1.1 %score.1 = (bf16[32,2048]{1,0:T(8,128)(2,1)S(1)}, f32[128,128]{1,0:T(8,128)S(1)}) custom-call(bf16[32,768]{1,0:T(8,128)(2,1)S(1)} %copy-done.1, bf16[2048,768]{1,0:T(8,128)(2,1)S(1)} %bitcast.11, f32[8,2048]{1,0:T(8,128)S(1)} %get-tuple-element.15.info_ref), custom_call_target="tpu_custom_call" | custom-call | tf_op jit(solution)/shard_map/score/pallas_call | solution.py:270
  71.9 14.5 %all_to_all.29 = f32[128,1,128]{2,1,0:T(1,128)S(1)} all-to-all(f32[128,1,128]{2,1,0:T(1,128)S(1)} %bitcast.17), channel_id=1, replica_groups=mesh['index'=8,'bulk'=16] {'index','bulk'}, dimensions={0} | all-to-all | bytes 131072 | tf_op jit(solution)/shard_map/all_to_all | solution.py:29
  86.4 1.3 %finish.1 = (f32[1,1]{1,0:T(1,128)}, f32[32,768]{1,0:T(8,128)}) custom-call(f32[128,128]{1,0:T(8,128)S(1)} %bitcast.15, bf16[32,2048]{1,0:T(8,128)(2,1)S(1)} %get-tuple-element.17.weights_ref, bf16[2048,768]{1,0:T(8,128)(2,1)S(1)} %bitcast.12), custom_call_target="tpu_custom_call" | custom-call | tf_op jit(solution)/shard_map/finish/pallas_call | solution.py:281
Async XLA Ops:
  0.6 22.6 %copy-start.2 = (f32[32,32]{1,0:T(8,128)S(1)}, f32[32,32]{1,0:T(8,128)}, u32[]{:S(2)}) copy-start(f32[32,32]{1,0:T(8,128)} %reader_ref.1) | copy-start | bytes 12292
  0.6 22.5 %copy-start = (bf16[2048,768]{1,0:T(8,128)(2,1)S(1)}, bf16[2048,768]{1,0:T(8,128)(2,1)}, u32[]{:S(2)}) copy-start(bf16[2048,768]{1,0:T(8,128)(2,1)} %passages_ref.1) | copy-start | bytes 9437188
  0.7 0.9 copy-start.3
  26.1 44.6 %copy-start.1 = (bf16[32,768]{1,0:T(8,128)(2,1)S(1)}, bf16[32,768]{1,0:T(8,128)(2,1)}, u32[]{:S(2)}) copy-start(bf16[32,768]{1,0:T(8,128)(2,1)} %questions_ref.1) | copy-start | bytes 147460

commit v13 on v12

--- a/solution.py
+++ b/solution.py
@@ -171,10 +171,11 @@
             moved[pl.ds(k, chunks, stride=STEP), :] = image[pl.ds(r, chunks, stride=STRIDE), :]
 
     def pack(line, moved):
-        for c in range(chunks):
-            rows_ref[line * LANES : (line + 1) * LANES, c * LANES : (c + 1) * LANES] = moved[
-                c * STEP : c * STEP + LANES, :
-            ].astype(rows_ref.dtype)
+        for g in range(0, LANES, 16):
+            block = [moved[c * STEP + g : c * STEP + g + 16, :] for c in range(chunks)]
+            rows_ref[line * LANES + g : line * LANES + g + 16, :] = jnp.concatenate(
+                block, axis=1
+            ).astype(rows_ref.dtype)
 
     buffers = (even, odd)
     move(0, even)

time: 87.9 us -> 87.7 us (level)
  no operation moved by 1% of the time
where the time goes in v13:
time: 87.7 us; the launch traced here: 87.5 us
  blocking collectives  80.2 us (91%)
  Pallas kernels  5.78 us (7%)
  local copies, waits for them, and re-layouts  0.88 us (1%)
    all_to_all x3, blocking collectives, exchange(): return lax.all_to_all(blocks, AXES, split_axis=0, concat_axis=0, tiled=True)  80.2 us
    pallas_call x1, Pallas kernels, body(): pl.pallas_call(fetch_kernel, out_shape=(pltpu.VMEM((slot_count, width), p...  2.79 us

profile of v13, /device:TPU:1, one launch (start us, length us, event | category | flops | bytes accessed | tf_op | source)
XLA Modules:
  0.0 87.5 jit_solution(290798277164007012)
XLA Ops:
  0.6 0.0 copy-start.2
  0.6 0.0 copy-start
  0.7 0.0 copy-start.3
  0.7 0.9 copy-done.3
  1.5 0.6 plan.1
  2.1 21.1 %all_to_all.27 = s32[128,1,128]{2,1,0:T(1,128)S(1)} all-to-all(s32[128,1,128]{2,1,0:T(1,128)S(1)} %bitcast.16), channel_id=1, replica_groups=mesh['index'=8,'bulk'=16] {'index','bulk'}, dimensions={0} | all-to-all | bytes 131072 | tf_op jit(solution)/shard_map/all_to_all | solution.py:29
  23.2 0.0 copy-done.2
  23.2 0.0 copy-done
  23.2 2.8 %fetch.1 = (bf16[2048,768]{1,0:T(8,128)(2,1)S(1)}, f32[8,2048]{1,0:T(8,128)S(1)}) custom-call(s32[128,128]{1,0:T(8,128)S(1)} %bitcast.14, bf16[2048,768]{1,0:T(8,128)(2,1)S(1)} %copy-done, s32[8,128]{1,0:T(8,128)S(1)} %get-tuple-element.12.ids_ref, f32[128,128]{1,0:T(8,128)S(1)} %get-tuple-element.13.places_ref, f32[32,32]{1,0:T(8,128)S(1)} %copy-done.2), custom_call_target="tpu_custom_call" | custom-call | tf_op jit(solution)/shard_map/fetch/pallas_call | solution.py:249
  26.0 0.0 copy-start.1
  26.0 44.6 %all_to_all.28 = bf16[128,16,768]{2,1,0:T(8,128)(2,1)S(1)} all-to-all(bf16[128,16,768]{2,1,0:T(8,128)(2,1)S(1)} %bitcast.13), channel_id=1, replica_groups=mesh['index'=8,'bulk'=16] {'index','bulk'}, dimensions={0} | all-to-all | bytes 6291456 | tf_op jit(solution)/shard_map/all_to_all | solution.py:29
  70.6 0.0 copy-done.1
  70.6 1.1 %score.1 = (bf16[32,2048]{1,0:T(8,128)(2,1)S(1)}, f32[128,128]{1,0:T(8,128)S(1)}) custom-call(bf16[32,768]{1,0:T(8,128)(2,1)S(1)} %copy-done.1, bf16[2048,768]{1,0:T(8,128)(2,1)S(1)} %bitcast.11, f32[8,2048]{1,0:T(8,128)S(1)} %get-tuple-element.15.info_ref), custom_call_target="tpu_custom_call" | custom-call | tf_op jit(solution)/shard_map/score/pallas_call | solution.py:271
  71.8 14.5 %all_to_all.29 = f32[128,1,128]{2,1,0:T(1,128)S(1)} all-to-all(f32[128,1,128]{2,1,0:T(1,128)S(1)} %bitcast.17), channel_id=1, replica_groups=mesh['index'=8,'bulk'=16] {'index','bulk'}, dimensions={0} | all-to-all | bytes 131072 | tf_op jit(solution)/shard_map/all_to_all | solution.py:29
  86.2 1.3 %finish.1 = (f32[1,1]{1,0:T(1,128)}, f32[32,768]{1,0:T(8,128)}) custom-call(f32[128,128]{1,0:T(8,128)S(1)} %bitcast.15, bf16[32,2048]{1,0:T(8,128)(2,1)S(1)} %get-tuple-element.17.weights_ref, bf16[2048,768]{1,0:T(8,128)(2,1)S(1)} %bitcast.12), custom_call_target="tpu_custom_call" | custom-call | tf_op jit(solution)/shard_map/finish/pallas_call | solution.py:282
Async XLA Ops:
  0.6 22.6 %copy-start.2 = (f32[32,32]{1,0:T(8,128)S(1)}, f32[32,32]{1,0:T(8,128)}, u32[]{:S(2)}) copy-start(f32[32,32]{1,0:T(8,128)} %reader_ref.1) | copy-start | bytes 12292
  0.6 22.5 %copy-start = (bf16[2048,768]{1,0:T(8,128)(2,1)S(1)}, bf16[2048,768]{1,0:T(8,128)(2,1)}, u32[]{:S(2)}) copy-start(bf16[2048,768]{1,0:T(8,128)(2,1)} %passages_ref.1) | copy-start | bytes 9437188
  0.7 0.9 copy-start.3
  26.0 44.6 %copy-start.1 = (bf16[32,768]{1,0:T(8,128)(2,1)S(1)}, bf16[32,768]{1,0:T(8,128)(2,1)}, u32[]{:S(2)}) copy-start(bf16[32,768]{1,0:T(8,128)(2,1)} %questions_ref.1) | copy-start | bytes 147460

commit v14 on v13

--- a/solution.py
+++ b/solution.py
@@ -202,7 +202,7 @@
     pieces = []
     for n in range(8):
         rows = rows_ref[n * block : (n + 1) * block, :]
-        pieces.append(inner(rows, questions).T if n % 2 else inner(questions, rows))
+        pieces.append(inner(questions, rows) if n % 2 else inner(rows, questions).T)
     scores = jnp.concatenate(pieces, axis=1) * scale
     log_reader = info_ref[1:2, :]
     reader = info_ref[2:3, :]

time: 87.7 us -> 87.8 us (level)
  no operation moved by 1% of the time
where the time goes in v14:
time: 87.8 us; the launch traced here: 87.6 us
  blocking collectives  80.2 us (91%)
  Pallas kernels  5.85 us (7%)
  local copies, waits for them, and re-layouts  0.88 us (1%)
    all_to_all x3, blocking collectives, exchange(): return lax.all_to_all(blocks, AXES, split_axis=0, concat_axis=0, tiled=True)  80.2 us
    pallas_call x1, Pallas kernels, body(): pl.pallas_call(fetch_kernel, out_shape=(pltpu.VMEM((slot_count, width), p...  2.79 us

profile of v14, /device:TPU:1, one launch (start us, length us, event | category | flops | bytes accessed | tf_op | source)
XLA Modules:
  0.0 87.6 jit_solution(6090217626928261085)
XLA Ops:
  0.6 0.0 copy-start.2
  0.6 0.0 copy-start
  0.7 0.0 copy-start.3
  0.7 0.9 copy-done.3
  1.5 0.6 plan.1
  2.1 21.1 %all_to_all.27 = s32[128,1,128]{2,1,0:T(1,128)S(1)} all-to-all(s32[128,1,128]{2,1,0:T(1,128)S(1)} %bitcast.16), channel_id=1, replica_groups=mesh['index'=8,'bulk'=16] {'index','bulk'}, dimensions={0} | all-to-all | bytes 131072 | tf_op jit(solution)/shard_map/all_to_all | solution.py:29
  23.2 0.0 copy-done.2
  23.2 0.0 copy-done
  23.2 2.8 %fetch.1 = (bf16[2048,768]{1,0:T(8,128)(2,1)S(1)}, f32[8,2048]{1,0:T(8,128)S(1)}) custom-call(s32[128,128]{1,0:T(8,128)S(1)} %bitcast.14, bf16[2048,768]{1,0:T(8,128)(2,1)S(1)} %copy-done, s32[8,128]{1,0:T(8,128)S(1)} %get-tuple-element.12.ids_ref, f32[128,128]{1,0:T(8,128)S(1)} %get-tuple-element.13.places_ref, f32[32,32]{1,0:T(8,128)S(1)} %copy-done.2), custom_call_target="tpu_custom_call" | custom-call | tf_op jit(solution)/shard_map/fetch/pallas_call | solution.py:249
  26.0 0.0 copy-start.1
  26.0 44.6 %all_to_all.28 = bf16[128,16,768]{2,1,0:T(8,128)(2,1)S(1)} all-to-all(bf16[128,16,768]{2,1,0:T(8,128)(2,1)S(1)} %bitcast.13), channel_id=1, replica_groups=mesh['index'=8,'bulk'=16] {'index','bulk'}, dimensions={0} | all-to-all | bytes 6291456 | tf_op jit(solution)/shard_map/all_to_all | solution.py:29
  70.6 0.0 copy-done.1
  70.6 1.2 %score.1 = (bf16[32,2048]{1,0:T(8,128)(2,1)S(1)}, f32[128,128]{1,0:T(8,128)S(1)}) custom-call(bf16[32,768]{1,0:T(8,128)(2,1)S(1)} %copy-done.1, bf16[2048,768]{1,0:T(8,128)(2,1)S(1)} %bitcast.11, f32[8,2048]{1,0:T(8,128)S(1)} %get-tuple-element.15.info_ref), custom_call_target="tpu_custom_call" | custom-call | tf_op jit(solution)/shard_map/score/pallas_call | solution.py:271
  71.8 14.5 %all_to_all.29 = f32[128,1,128]{2,1,0:T(1,128)S(1)} all-to-all(f32[128,1,128]{2,1,0:T(1,128)S(1)} %bitcast.17), channel_id=1, replica_groups=mesh['index'=8,'bulk'=16] {'index','bulk'}, dimensions={0} | all-to-all | bytes 131072 | tf_op jit(solution)/shard_map/all_to_all | solution.py:29
  86.3 1.3 %finish.1 = (f32[1,1]{1,0:T(1,128)}, f32[32,768]{1,0:T(8,128)}) custom-call(f32[128,128]{1,0:T(8,128)S(1)} %bitcast.15, bf16[32,2048]{1,0:T(8,128)(2,1)S(1)} %get-tuple-element.17.weights_ref, bf16[2048,768]{1,0:T(8,128)(2,1)S(1)} %bitcast.12), custom_call_target="tpu_custom_call" | custom-call | tf_op jit(solution)/shard_map/finish/pallas_call | solution.py:282
Async XLA Ops:
  0.6 22.6 %copy-start.2 = (f32[32,32]{1,0:T(8,128)S(1)}, f32[32,32]{1,0:T(8,128)}, u32[]{:S(2)}) copy-start(f32[32,32]{1,0:T(8,128)} %reader_ref.1) | copy-start | bytes 12292
  0.6 22.5 %copy-start = (bf16[2048,768]{1,0:T(8,128)(2,1)S(1)}, bf16[2048,768]{1,0:T(8,128)(2,1)}, u32[]{:S(2)}) copy-start(bf16[2048,768]{1,0:T(8,128)(2,1)} %passages_ref.1) | copy-start | bytes 9437188
  0.7 0.9 copy-start.3
  26.0 44.6 %copy-start.1 = (bf16[32,768]{1,0:T(8,128)(2,1)S(1)}, bf16[32,768]{1,0:T(8,128)(2,1)}, u32[]{:S(2)}) copy-start(bf16[32,768]{1,0:T(8,128)(2,1)} %questions_ref.1) | copy-start | bytes 147460
